TPU v7x, 32 devices: a whole 2x2x4 slice. The times are simulated.
32 devices in a mesh: groups: 2 (over y), seq: 8 (over z, x), ch: 2 (over core).
Axes of the slice: x: 2, y: 2, z: 4, core: 2. Of those that a mesh axis runs over, the one named last changes fastest.
Arguments:
- tokens: int32 [4096], P(('groups', 'seq')), parts along dimension 0, may hold values from 0 to 3
- nuc_table: bfloat16 [3, 4, 4096], P(None, None, 'ch'), may hold values from -6 to 6
- short_filter: float32 [3, 7, 4096], P(None, None, 'ch'), may hold values from -2 to 2
- mr_filter: float32 [256, 128], P('ch'), may hold values from -0.5 to 0.5
- head_weight: bfloat16 [5, 4096, 256], P(None, 'ch'), may hold values from -0.03125 to 0.03125
Outputs:
- annotation: bfloat16 [4096, 256], P(('groups', 'seq')), parts along dimension 0
There are 2 independent parts, one for each index of `groups`. A program takes and returns all parts, laid end to end along the dimension named above; an argument that names none is the same for every part. Nothing has to cross between parts.
Inputs may be any that keep to these rules, and one draw needn't show every extreme that they name: `tokens`: each entry is a nucleotide letter: 0 A, 1 C, 2 G, 3 T; the complement of a is 3 - a. The letters are integers, so they may cross devices packed several to a 16-bit or wider word without losing anything.
All inputs are finite; a program needn't handle non-finite values.
Results may differ from a plain program's by a relative error of at most 0.0049.
Values may be sent and summed in bfloat16 or wider, within the bound.
No kernel may reach another device: no remote copies, remote signals or barrier semaphores. Data moves between devices by JAX's collectives and lax.ppermute only.
A program may use at most 128 MiB of HBM per device.

v0:
```python
import functools

import jax
import jax.numpy as jnp
from jax import lax
from jax.experimental import pallas as pl
from jax.experimental.pallas import tpu as pltpu
from jax.sharding import PartitionSpec as P

LANES = 128
HALF = 64
LETTERS = 4
STRANDS = 2
PARTS = 2
WINDOWS = STRANDS * PARTS
F32 = jnp.float32
BF16 = jnp.bfloat16


def up(value, step):
    return -(-value // step) * step


def iota(shape, dim):
    return lax.broadcasted_iota(jnp.int32, shape, dim)


def dot(a, b):
    return jnp.dot(a, b, preferred_element_type=F32)


def flip_matrix(size):
    return (iota((size, size), 0) + iota((size, size), 1) == size - 1).astype(F32).astype(BF16)


def build_onehot(tok_ref, oh_ref, short_len, window, seg_rows, query_shift, query_rows):
    tok = tok_ref[...]
    width = tok.shape[1]

    def shifted(amount, count):
        return pltpu.roll(tok, (width - amount) % width, 1)[:, :count]

    lags = []
    for lag in range(short_len):
        lead = short_len - lag
        lags.append(
            jnp.concatenate(
                [
                    shifted(lead, window),
                    shifted(lead - 1, LANES),
                    shifted(lead + query_shift, query_rows),
                ],
                axis=1,
            )
        )
    own = lags[0] > 0
    zero = jnp.zeros_like(lags[0])
    lags = [jnp.where(own, lag, zero) for lag in lags]
    while len(lags) % 2:
        lags.append(zero)
    total = lags[0].shape[1]
    row = iota((2 * LETTERS, total), 0)
    first = row < LETTERS
    letter = jnp.where(first, row, row - LETTERS) + 1
    blocks = []
    for x in range(WINDOWS):
        pieces = []
        for pair in range(len(lags) // 2):
            a = jnp.broadcast_to(lags[2 * pair][x : x + 1], (2 * LETTERS, total))
            b = jnp.broadcast_to(lags[2 * pair + 1][x : x + 1], (2 * LETTERS, total))
            pieces.append((jnp.where(first, a, b) == letter).astype(F32))
        blocks += pieces + pieces
    oh_ref[...] = jnp.concatenate(blocks, axis=0).T.astype(BF16)


def build_weights(nuc_ref, sf_ref, wn_ref, short_len):
    row = iota((2 * LETTERS, LANES), 0)
    first = row < LETTERS
    pairs = (short_len + 1) // 2

    def step(v, carry):
        lanes = pl.ds(pl.multiple_of(v * LANES, LANES), LANES)
        for m in range(3):
            nuc = nuc_ref[m, :, lanes].astype(F32)
            nuc = jnp.concatenate([nuc, nuc], axis=0)
            taps = sf_ref[m, :, lanes]
            pieces = []
            for pair in range(pairs):
                a = jnp.broadcast_to(taps[2 * pair : 2 * pair + 1], row.shape)
                if 2 * pair + 1 < short_len:
                    b = jnp.broadcast_to(taps[2 * pair + 1 : 2 * pair + 2], row.shape)
                else:
                    b = jnp.zeros(row.shape, F32)
                pieces.append(jnp.where(first, a, b) * nuc)
            product = jnp.concatenate(pieces, axis=0)
            high = product.astype(BF16).astype(F32)
            full = jnp.concatenate([high, product - high], axis=0)
            turned = pltpu.roll(full, HALF, 1)
            low_half = iota(full.shape, 1) < HALF
            zero = jnp.zeros_like(full)
            wn_ref[m, 0, :, lanes] = jnp.where(low_half, full, zero).astype(BF16)
            wn_ref[m, 1, :, lanes] = jnp.where(low_half, zero, turned).astype(BF16)
            wn_ref[m, 2, :, lanes] = jnp.where(low_half, zero, full).astype(BF16)
            wn_ref[m, 3, :, lanes] = jnp.where(low_half, turned, zero).astype(BF16)
        return carry

    lax.fori_loop(0, nuc_ref.shape[2] // LANES, step, 0)


def toeplitz(reverse_row, rows):
    taps = reverse_row.shape[1]
    turned = pltpu.roll(jnp.broadcast_to(reverse_row, (taps, taps)), 0, 1, stride=1, stride_axis=0)
    turned = jnp.concatenate([turned, turned[: rows - taps]], axis=0)
    gap = iota((rows, taps), 0) - iota((rows, taps), 1)
    zero = jnp.zeros_like(turned)
    near = jnp.where((gap <= 1) & (gap >= 2 - taps), turned, zero)
    far = jnp.where(gap >= 2, turned, zero)
    return jnp.concatenate([near, far], axis=1).astype(BF16)


def kernel(
    sizes, tok_ref, nuc_ref, sf_ref, mr_ref, hw_hbm, out_ref,
    oh_ref, wn_ref, fr_ref, track_ref, hw_ref, ps_ref, sem,
):
    rows, short_len, taps, group_width, head_taps = sizes
    channels = nuc_ref.shape[2]
    window = 2 * taps
    part_rows = (rows + head_taps - 1) // PARTS
    track_rows = up(part_rows, 16)
    query_shift = taps - 2
    query_rows = up(track_rows, LANES)

    fetch = pltpu.make_async_copy(hw_hbm, hw_ref, sem)
    fetch.start()

    build_onehot(tok_ref, oh_ref, short_len, window, LANES, query_shift, query_rows)
    build_weights(nuc_ref, sf_ref, wn_ref, short_len)
    place = iota((taps, taps), 0) + iota((taps, taps), 1)
    turn = (place == taps - 2) | (place == 2 * taps - 2)
    fr_ref[...] = dot(mr_ref[...].astype(BF16), turn.astype(F32).astype(BF16))

    groups_in_half = HALF // group_width
    lane_group = (iota((track_rows, 2 * LANES), 1) % HALF) // group_width
    fix_group = lane_group[:8]
    fix_row = iota((8, 2 * LANES), 0) == 0

    def step(v, carry):
        lanes = pl.ds(pl.multiple_of(v * LANES, LANES), LANES)
        per_step = LANES // group_width
        taps_rev = fr_ref[pl.ds(pl.multiple_of(v * per_step, per_step), per_step), :]
        kv_hot = oh_ref[: window + 16, :]
        q_hot = oh_ref[window + LANES : window + LANES + track_rows, :]
        products = []
        for half in range(2):
            def weights(m):
                a = wn_ref[m, 2 * half, :, lanes]
                b = wn_ref[m, 2 * half + 1, :, lanes]
                z = jnp.zeros_like(a)
                left = jnp.concatenate([a, b, z, z], axis=0)
                right = jnp.concatenate([z, z, a, b], axis=0)
                return jnp.concatenate([left, right], axis=1)

            gated = dot(kv_hot, weights(1)) * dot(kv_hot, weights(2))
            query = dot(q_hot, weights(0))
            data = gated[:window].astype(BF16)
            before = jnp.broadcast_to(gated[window : window + 1], fix_row.shape)
            mixed = None
            fix = None
            for g in range(groups_in_half):
                index = half * groups_in_half + g
                taps_row = taps_rev[index : index + 1]
                piece = dot(toeplitz(taps_row, track_rows), data)
                last = jnp.broadcast_to(taps_row[:, taps - 1 :], fix_row.shape)
                mixed = piece if g == 0 else jnp.where(lane_group == g, piece, mixed)
                fix = last if g == 0 else jnp.where(fix_group == g, last, fix)
            fix = jnp.where(fix_row, fix * before, 0.0)
            mixed = jnp.concatenate([mixed[:8] + fix, mixed[8:]], axis=0)
            products.append(query * mixed)
        low_half = iota((track_rows, LANES), 1) < HALF
        for n in range(2):
            a = products[0][:, n * LANES : (n + 1) * LANES]
            b = products[1][:, n * LANES : (n + 1) * LANES]
            even = jnp.where(low_half, a, b)
            odd = pltpu.roll(jnp.where(low_half, b, a), HALF, 1)
            at = 2 * n * track_rows
            track_ref[at : at + track_rows, lanes] = even.astype(BF16)
            track_ref[at + track_rows : at + 2 * track_rows, lanes] = odd.astype(BF16)
        return carry

    lax.fori_loop(0, channels // LANES, step, 0)

    fetch.wait()
    totals = [None, None]
    for k in range(head_taps):
        score = dot(track_ref[...], hw_ref[k])
        for s in range(STRANDS):
            at = 2 * s * track_rows
            ps_ref[s, :track_rows] = score[at : at + track_rows]
            ps_ref[s, part_rows : part_rows + track_rows] = score[at + track_rows : at + 2 * track_rows]
            part = ps_ref[s, k : k + rows]
            totals[s] = part if k == 0 else totals[s] + part
    forward, backward = totals
    flip = flip_matrix(rows)
    for _ in range(3):
        high = backward.astype(BF16)
        forward = forward + dot(flip, high)
        backward = backward - high.astype(F32)
    out_ref[...] = forward


def shards(tokens, nuc_table, short_filter, mr_filter, head_weight):
    rows = tokens.shape[0]
    _, short_len, channels = short_filter.shape
    filters, taps = mr_filter.shape
    head_taps, _, outs = head_weight.shape
    rim = (head_taps - 1) // 2
    reach = taps - 1 + short_len - 1 + rim
    part_rows = (rows + 2 * rim) // PARTS
    window = 2 * taps
    width = up(window + short_len, LANES)
    count = lax.axis_size("seq")

    coded = tokens + 1
    before = lax.ppermute(coded[rows - reach :], "seq", [(i, i + 1) for i in range(count - 1)])
    after = lax.ppermute(coded[:reach], "seq", [(i + 1, i) for i in range(count - 1)])
    forward = jnp.concatenate([before, coded, after])
    backward = jnp.where(forward > 0, LETTERS + 1 - forward, 0)[::-1]
    lanes = []
    for strand in (forward, backward):
        for n in range(PARTS):
            lanes.append(strand[n * part_rows : n * part_rows + width])
    lanes += [jnp.zeros_like(lanes[0])] * (8 - WINDOWS)
    letters = jnp.stack(lanes)

    track_rows = up(part_rows, 16)
    hot_rows = window + LANES + up(track_rows, LANES)
    hot_depth = WINDOWS * 2 * LETTERS * up(short_len, 2)
    vmem = pl.BlockSpec(memory_space=pltpu.VMEM)
    partial = pl.pallas_call(
        functools.partial(kernel, (rows, short_len, taps, channels // filters, head_taps)),
        out_shape=jax.ShapeDtypeStruct((rows, outs), F32),
        in_specs=[vmem, vmem, vmem, vmem, pl.BlockSpec(memory_space=pl.ANY)],
        out_specs=vmem,
        scratch_shapes=[
            pltpu.VMEM((hot_rows, hot_depth), BF16),
            pltpu.VMEM((3, 4, hot_depth // WINDOWS, channels), BF16),
            pltpu.VMEM((filters, taps), F32),
            pltpu.VMEM((WINDOWS * track_rows, channels), BF16),
            pltpu.VMEM(head_weight.shape, BF16),
            pltpu.VMEM((STRANDS, part_rows + track_rows + 6, outs), F32),
            pltpu.SemaphoreType.DMA,
        ],
        compiler_params=pltpu.CompilerParams(vmem_limit_bytes=40 * 1024 * 1024),
        cost_estimate=pl.CostEstimate(
            flops=2 * 4 * 10**9, bytes_accessed=8 * 10**6, transcendentals=0
        ),
    )(letters, nuc_table, short_filter, mr_filter, head_weight)

    cores = lax.axis_size("ch")
    ring = [(i, (i + 1) % cores) for i in range(cores)]
    total, moving = partial, partial
    for _ in range(cores - 1):
        moving = lax.ppermute(moving, "ch", ring)
        total = total + moving
    return total.astype(BF16)


def solution(mesh):
    in_specs = (
        P(("groups", "seq")),
        P(None, None, "ch"),
        P(None, None, "ch"),
        P("ch", None),
        P(None, "ch", None),
    )
    out_specs = P(("groups", "seq"), None)
    return jax.shard_map(shards, mesh=mesh, in_specs=in_specs, out_specs=out_specs, check_vma=False)
```

profile of v0, /device:TPU:0, one launch (start us, length us, event | category | flops | bytes accessed | tf_op | source)
XLA Modules:
  0.0 38.7 jit_solution(12267426369425375811)
XLA Ops:
  0.0 0.7 %broadcast_add_fusion = s32[256]{0:T(256)S(1)} fusion(s32[256]{0:T(256)} %param.5), kind=kLoop, calls=%fused_computation.4 | loop fusion | flops 256 | bytes 2048 | tf_op jit(solution)/shard_map/add | solution.py:223
  0.7 0.1 fusion.1
  0.8 4.9 %collective-permute-start = (s32[135]{0:T(256)S(1)}, s32[135]{0:T(256)S(1)}, u32[]{:S(2)}, u32[]{:S(2)}) collective-permute-start(s32[135]{0:T(256)S(1)} %get-tuple-element.10), channel_id=1, source_target_pairs={{0,2},{2,4},{4,6},{6,8},{8,10},{10,12},{12,14},{1,3},{3,5},{5,7},{... | collective-permute-start | bytes 1628 | tf_op jit(solution)/shard_map/ppermute | solution.py:224
  5.6 1.3 %collective-permute-start.1 = (s32[135]{0:T(256)S(1)}, s32[135]{0:T(256)S(1)}, u32[]{:S(2)}, u32[]{:S(2)}) collective-permute-start(s32[135]{0:T(256)S(1)} %get-tuple-element.9), channel_id=1, source_target_pairs={{2,0},{4,2},{6,4},{8,6},{10,8},{12,10},{14,12},{3,1},{5,3},{7,5},{... | collective-permute-start | bytes 1628 | tf_op jit(solution)/shard_map/ppermute | solution.py:225
  6.9 0.0 collective-permute-done
  6.9 0.1 pad_add_fusion.1
  7.0 4.1 %collective-permute-done.1 = s32[135]{0:T(256)S(1)} collective-permute-done((s32[135]{0:T(256)S(1)}, s32[135]{0:T(256)S(1)}, u32[]{:S(2)}, u32[]{:S(2)}) %collective-permute-start.1) | collective-permute-done | bytes 572 | tf_op jit(solution)/shard_map/ppermute | solution.py:225
  11.1 0.1 subtract_select_fusion
  11.2 0.1 fusion
  11.2 0.1 slice.32
  11.3 0.1 slice.30
  11.5 0.1 slice.28
  11.6 0.0 copy-start
  11.6 2.5 %copy-done = bf16[5,2048,256]{2,1,0:T(8,128)(2,1)S(1)} copy-done((bf16[5,2048,256]{2,1,0:T(8,128)(2,1)S(1)}, bf16[5,2048,256]{2,1,0:T(8,128)(2,1)}, u32[]{:S(2)}) %copy-start) | copy-done | bytes 5242904
  14.1 0.0 copy-start.1
  14.1 0.9 %copy-done.1 = f32[3,7,2048]{2,1,0:T(8,128)S(1)} copy-done((f32[3,7,2048]{2,1,0:T(8,128)S(1)}, f32[3,7,2048]{2,1,0:T(8,128)}, u32[]{:S(2)}) %copy-start.1) | copy-done | bytes 172056
  15.0 0.0 copy-start.2
  15.0 0.8 %copy-done.2 = f32[128,128]{1,0:T(8,128)S(1)} copy-done((f32[128,128]{1,0:T(8,128)S(1)}, f32[128,128]{1,0:T(8,128)}, u32[]{:S(2)}) %copy-start.2) | copy-done | bytes 65560
  15.8 0.0 copy-start.3
  15.8 0.8 %copy-done.3 = bf16[3,4,2048]{2,1,0:T(4,128)(2,1)S(1)} copy-done((bf16[3,4,2048]{2,1,0:T(4,128)(2,1)S(1)}, bf16[3,4,2048]{2,1,0:T(4,128)(2,1)}, u32[]{:S(2)}) %copy-start.3) | copy-done | bytes 49176
  16.6 19.7 %shard_map.55 = f32[256,256]{1,0:T(8,128)S(1)} custom-call(s32[8,384]{1,0:T(8,128)S(1)} %stack.23.tok_ref, bf16[3,4,2048]{2,1,0:T(4,128)(2,1)S(1)} %copy-done.3, f32[3,7,2048]{2,1,0:T(8,128)S(1)} %copy-done.1, f32[128,128]{1,0:T(8,128)S(1)} %copy-done.2, bf16[5,2048,256]{2,1,0:T(8,128)(2,1)S(1)} %copy-done), custom_call_target="tpu_custom_call" | custom-call | flops 8000000000 | bytes 8000000 | tf_op jit(solution)/shard_map/pallas_call | solution.py:239
  36.4 0.1 collective-permute-start.2
  36.5 1.5 %collective-permute-done.2 = f32[256,256]{1,0:T(8,128)S(1)} collective-permute-done((f32[256,256]{1,0:T(8,128)S(1)}, f32[256,256]{1,0:T(8,128)S(1)}, u32[]{:S(2)}, u32[]{:S(2)}) %collective-permute-start.2) | collective-permute-done | bytes 262176 | tf_op jit(solution)/shard_map/ppermute | solution.py:263
  38.0 0.7 %add_convert_fusion = bf16[256,256]{1,0:T(8,128)(2,1)} fusion(f32[256,256]{1,0:T(8,128)S(1)} %shard_map.55, f32[256,256]{1,0:T(8,128)S(1)} %collective-permute-done.2), kind=kLoop, calls=%fused_computation | loop fusion | flops 131072 | bytes 655360 | tf_op jit(solution)/shard_map/convert_element_type | solution.py:265
  (6 shorter events, 0.1 us)
Async XLA Ops:
  0.8 6.2 %collective-permute-start = (s32[135]{0:T(256)S(1)}, s32[135]{0:T(256)S(1)}, u32[]{:S(2)}, u32[]{:S(2)}) collective-permute-start(s32[135]{0:T(256)S(1)} %get-tuple-element.10), channel_id=1, source_target_pairs={{0,2},{2,4},{4,6},{6,8},{8,10},{10,12},{12,14},{1,3},{3,5},{5,7},{... | collective-permute-start | bytes 1628 | tf_op jit(solution)/shard_map/ppermute | solution.py:224
  5.6 5.5 %collective-permute-start.1 = (s32[135]{0:T(256)S(1)}, s32[135]{0:T(256)S(1)}, u32[]{:S(2)}, u32[]{:S(2)}) collective-permute-start(s32[135]{0:T(256)S(1)} %get-tuple-element.9), channel_id=1, source_target_pairs={{2,0},{4,2},{6,4},{8,6},{10,8},{12,10},{14,12},{3,1},{5,3},{7,5},{... | collective-permute-start | bytes 1628 | tf_op jit(solution)/shard_map/ppermute | solution.py:225
  11.6 2.5 %copy-start = (bf16[5,2048,256]{2,1,0:T(8,128)(2,1)S(1)}, bf16[5,2048,256]{2,1,0:T(8,128)(2,1)}, u32[]{:S(2)}) copy-start(bf16[5,2048,256]{2,1,0:T(8,128)(2,1)} %hw_hbm.1) | copy-start | bytes 15728644
  14.1 0.9 %copy-start.1 = (f32[3,7,2048]{2,1,0:T(8,128)S(1)}, f32[3,7,2048]{2,1,0:T(8,128)}, u32[]{:S(2)}) copy-start(f32[3,7,2048]{2,1,0:T(8,128)} %sf_ref.1) | copy-start | bytes 516100
  15.0 0.8 %copy-start.2 = (f32[128,128]{1,0:T(8,128)S(1)}, f32[128,128]{1,0:T(8,128)}, u32[]{:S(2)}) copy-start(f32[128,128]{1,0:T(8,128)} %mr_ref.1) | copy-start | bytes 196612
  15.8 0.8 %copy-start.3 = (bf16[3,4,2048]{2,1,0:T(4,128)(2,1)S(1)}, bf16[3,4,2048]{2,1,0:T(4,128)(2,1)}, u32[]{:S(2)}) copy-start(bf16[3,4,2048]{2,1,0:T(4,128)(2,1)} %nuc_ref.1) | copy-start | bytes 147460
  36.4 1.6 %collective-permute-start.2 = (f32[256,256]{1,0:T(8,128)S(1)}, f32[256,256]{1,0:T(8,128)S(1)}, u32[]{:S(2)}, u32[]{:S(2)}) collective-permute-start(f32[256,256]{1,0:T(8,128)S(1)} %shard_map.55), channel_id=1, source_target_pairs={{0,1},{1,0},{2,3},{3,2},{4,5},{5,4},{6,7},{7,6},{8,9},{9,8},{10,11... | collective-permute-start | bytes 786440 | tf_op jit(solution)/shard_map/ppermute | solution.py:263
where the time goes:
time: 39 us; the launch traced here: 38.7 us
  Pallas kernels  19.7 us (51%)
  starting transfers between devices  6.22 us (16%)
  waiting for transfers between devices  5.6 us (14%)
  local copies, waits for them, and re-layouts  5.51 us (14%)
  other arithmetic  1.52 us (4%)
    pallas_call x1, Pallas kernels, shards(): pl.pallas_call(functools.partial(kernel, (rows, short_len, taps, channels...  19.7 us
    unnamed x8, local copies, waits for them, and re-layouts  5.05 us
    ppermute x1, starting transfers between devices, shards(): lax.ppermute(coded[rows - reach:], 'seq', [(i, i + 1) for i in range(coun...  4.86 us
    ppermute x1, waiting for transfers between devices, shards(): lax.ppermute(coded[:reach], 'seq', [(i + 1, i) for i in range(count - 1)])  4.07 us
    ppermute x1, waiting for transfers between devices, shards(): moving = lax.ppermute(moving, 'ch', ring)  1.52 us
    ppermute x1, starting transfers between devices, shards(): lax.ppermute(coded[:reach], 'seq', [(i + 1, i) for i in range(count - 1)])  1.29 us
  transfers between devices with their start and end apart: 3, of which 2 were waited for; matrix products, arithmetic and copies ran while one was open for 0% of the time, Pallas kernels for 0%

commit v1 on v0

v1 whole, which is shorter than its diff:
```python
import functools

import jax
import jax.numpy as jnp
from jax import lax
from jax.experimental import pallas as pl
from jax.experimental.pallas import tpu as pltpu
from jax.sharding import PartitionSpec as P

LANES = 128
HALF = 64
WIDE = 256
LETTERS = 4
STRANDS = 2
PARTS = 2
WINDOWS = STRANDS * PARTS
F32 = jnp.float32
BF16 = jnp.bfloat16


def up(value, step):
    return -(-value // step) * step


def iota(shape, dim):
    return lax.broadcasted_iota(jnp.int32, shape, dim)


def dot(a, b):
    return jnp.dot(a, b, preferred_element_type=F32)


def flip_matrix(size):
    return (iota((size, size), 0) + iota((size, size), 1) == size - 1).astype(F32).astype(BF16)


def build_onehot(tok_ref, hot_ref, query_ref, short_len, window, query_shift):
    tok = tok_ref[...]
    width = tok.shape[1]
    hot_rows = hot_ref.shape[0] // WINDOWS
    query_rows = query_ref.shape[0] // WINDOWS
    query_lanes = up(query_rows, LANES)

    def shifted(amount, count):
        return pltpu.roll(tok, (width - amount) % width, 1)[:, :count]

    lags = []
    for lag in range(short_len):
        lead = short_len - lag
        lags.append(
            jnp.concatenate(
                [
                    shifted(lead, window),
                    shifted(lead - 1, LANES),
                    shifted(lead + query_shift, query_lanes),
                ],
                axis=1,
            )
        )
    own = lags[0] > 0
    zero = jnp.zeros_like(lags[0])
    lags = [jnp.where(own, lag, zero) for lag in lags]
    while len(lags) % 2:
        lags.append(zero)
    total = lags[0].shape[1]
    row = iota((2 * LETTERS, total), 0)
    first = row < LETTERS
    letter = jnp.where(first, row, row - LETTERS) + 1
    for x in range(WINDOWS):
        pieces = []
        for pair in range(len(lags) // 2):
            a = jnp.broadcast_to(lags[2 * pair][x : x + 1], (2 * LETTERS, total))
            b = jnp.broadcast_to(lags[2 * pair + 1][x : x + 1], (2 * LETTERS, total))
            pieces.append((jnp.where(first, a, b) == letter).astype(F32))
        hot = jnp.concatenate(pieces + pieces, axis=0).T.astype(BF16)
        hot_ref[x * hot_rows : (x + 1) * hot_rows] = hot[:hot_rows]
        at = window + LANES
        query_ref[x * query_rows : (x + 1) * query_rows] = hot[at : at + query_rows]


def build_weights(nuc_ref, sf_ref, wn_ref, short_len):
    row = iota((2 * LETTERS, WIDE), 0)
    first = row < LETTERS
    pairs = (short_len + 1) // 2

    def step(v, carry):
        lanes = pl.ds(pl.multiple_of(v * WIDE, WIDE), WIDE)
        for m in range(3):
            nuc = nuc_ref[m, :, lanes].astype(F32)
            nuc = jnp.concatenate([nuc, nuc], axis=0)
            taps = sf_ref[m, :, lanes]
            pieces = []
            for pair in range(pairs):
                a = jnp.broadcast_to(taps[2 * pair : 2 * pair + 1], row.shape)
                if 2 * pair + 1 < short_len:
                    b = jnp.broadcast_to(taps[2 * pair + 1 : 2 * pair + 2], row.shape)
                else:
                    b = jnp.zeros(row.shape, F32)
                pieces.append(jnp.where(first, a, b) * nuc)
            product = jnp.concatenate(pieces, axis=0)
            high = product.astype(BF16)
            low = (product - high.astype(F32)).astype(BF16)
            wn_ref[m, :, lanes] = jnp.concatenate([high, low], axis=0)
        return carry

    lax.fori_loop(0, nuc_ref.shape[2] // WIDE, step, 0)


def toeplitz(reverse_row, rows):
    taps = reverse_row.shape[1]
    turned = pltpu.roll(jnp.broadcast_to(reverse_row, (taps, taps)), 0, 1, stride=1, stride_axis=0)
    turned = jnp.concatenate([turned, turned[: rows - taps]], axis=0)
    gap = iota((rows, taps), 0) - iota((rows, taps), 1)
    zero = jnp.zeros_like(turned)
    near = jnp.where((gap <= 1) & (gap >= 2 - taps), turned, zero)
    far = jnp.where(gap >= 2, turned, zero)
    return jnp.concatenate([near, far], axis=1).astype(BF16)


def kernel(
    sizes, tok_ref, nuc_hbm, sf_hbm, mr_hbm, hw_hbm, out_ref,
    nuc_ref, sf_ref, mr_ref, hw_ref, hot_ref, query_ref, wn_ref, fr_ref, track_ref, ps_ref, sems,
):
    rows, short_len, taps, group_width, head_taps = sizes
    channels = nuc_ref.shape[2]
    window = 2 * taps
    part_rows = (rows + head_taps - 1) // PARTS
    track_rows = up(part_rows, 16)
    used_rows = window + 8
    hot_rows = window + 16

    pairs = [(nuc_hbm, nuc_ref), (sf_hbm, sf_ref), (mr_hbm, mr_ref), (hw_hbm, hw_ref)]
    copies = [pltpu.make_async_copy(a, b, sems.at[i]) for i, (a, b) in enumerate(pairs)]
    for copy in copies:
        copy.start()
    fetch = copies[-1]

    build_onehot(tok_ref, hot_ref, query_ref, short_len, window, taps - 2)
    for copy in copies[:-1]:
        copy.wait()
    build_weights(nuc_ref, sf_ref, wn_ref, short_len)
    place = iota((taps, taps), 0) + iota((taps, taps), 1)
    turn = (place == taps - 2) | (place == 2 * taps - 2)
    fr_ref[...] = dot(mr_ref[...].astype(BF16), turn.astype(F32).astype(BF16))

    tile_groups = HALF // group_width
    lane_group = (iota((track_rows, WIDE), 1) % HALF) // group_width
    fix_group = lane_group[:8]
    fix_row = iota((8, WIDE), 0) == 0

    def mix(taps_rows, merged):
        data = merged[:window].astype(BF16)
        before = jnp.broadcast_to(merged[window : window + 1], fix_row.shape)
        mixed = None
        fix = None
        for g in range(tile_groups):
            taps_row = taps_rows[g : g + 1]
            piece = dot(toeplitz(taps_row, track_rows), data)
            last = jnp.broadcast_to(taps_row[:, taps - 1 :], fix_row.shape)
            mixed = piece if g == 0 else jnp.where(lane_group == g, piece, mixed)
            fix = last if g == 0 else jnp.where(fix_group == g, last, fix)
        fix = jnp.where(fix_row, fix * before, 0.0)
        return jnp.concatenate([mixed[:8] + fix, mixed[8:]], axis=0)

    def step(v, carry):
        lanes = pl.ds(pl.multiple_of(v * WIDE, WIDE), WIDE)
        per_step = WIDE // group_width
        taps_rev = fr_ref[pl.ds(pl.multiple_of(v * per_step, per_step), per_step), :]
        hot = hot_ref[...]
        gated = dot(hot, wn_ref[1, :, lanes]) * dot(hot, wn_ref[2, :, lanes])
        query = dot(query_ref[...], wn_ref[0, :, lanes])
        low_half = iota((used_rows, LANES), 1) < HALF
        low_track = low_half[:track_rows]
        for j in range(2):
            column = gated[:, j * LANES : (j + 1) * LANES]
            part = [column[x * hot_rows : x * hot_rows + used_rows] for x in range(WINDOWS)]
            lower, upper = [], []
            for x in range(0, WINDOWS, 2):
                turned = pltpu.roll(part[x + 1], HALF, 1)
                lower.append(jnp.where(low_half, part[x], turned))
                upper.append(jnp.where(low_half, turned, part[x]))
            at = 2 * j * tile_groups
            lower = mix(taps_rev[at : at + tile_groups], jnp.concatenate(lower, axis=1))
            upper = mix(taps_rev[at + tile_groups : at + 2 * tile_groups], jnp.concatenate(upper, axis=1))
            to = pl.ds(pl.multiple_of(v * WIDE + j * LANES, LANES), LANES)
            for x in range(0, WINDOWS, 2):
                a = lower[:, x * HALF : x * HALF + LANES]
                b = upper[:, x * HALF : x * HALF + LANES]
                even = jnp.where(low_track, a, b)
                odd = pltpu.roll(jnp.where(low_track, b, a), HALF, 1)
                for y, mixed in ((x, even), (x + 1, odd)):
                    at = y * track_rows
                    own = query[at : at + track_rows, j * LANES : (j + 1) * LANES]
                    track_ref[at : at + track_rows, to] = (own * mixed).astype(BF16)
        return carry

    lax.fori_loop(0, channels // WIDE, step, 0)

    fetch.wait()
    totals = [None, None]
    for k in range(head_taps):
        score = dot(track_ref[...], hw_ref[k])
        for s in range(STRANDS):
            at = 2 * s * track_rows
            ps_ref[s, :track_rows] = score[at : at + track_rows]
            ps_ref[s, part_rows : part_rows + track_rows] = score[at + track_rows : at + 2 * track_rows]
            part = ps_ref[s, k : k + rows]
            totals[s] = part if k == 0 else totals[s] + part
    forward, backward = totals
    flip = flip_matrix(rows)
    for _ in range(3):
        high = backward.astype(BF16)
        forward = forward + dot(flip, high)
        backward = backward - high.astype(F32)
    out_ref[...] = forward


def neighbour_ways(count, cores):
    ways = []
    for i in range(count):
        for c in range(cores):
            step = 1 if (i + c) % 2 == 0 else -1
            there = (i + step, c ^ 1) if 0 <= i + step < count else (i, c ^ 1)
            ways.append((i * cores + c, there[0] * cores + there[1]))
    return ways


def shards(tokens, nuc_table, short_filter, mr_filter, head_weight):
    rows = tokens.shape[0]
    _, short_len, channels = short_filter.shape
    filters, taps = mr_filter.shape
    head_taps, _, outs = head_weight.shape
    rim = (head_taps - 1) // 2
    reach = taps - 1 + short_len - 1 + rim
    part_rows = (rows + 2 * rim) // PARTS
    window = 2 * taps
    width = up(window + short_len, LANES)
    count = lax.axis_size("seq")

    cores = lax.axis_size("ch")
    place = lax.axis_index("seq")
    ways = neighbour_ways(count, cores)
    one = lax.ppermute(tokens, ("seq", "ch"), ways)
    two = lax.ppermute(tokens, ("seq", "ch"), [(b, a) for a, b in ways])
    onward = (place + lax.axis_index("ch")) % 2 == 0
    before = jnp.where(onward, one, two)[rows - reach :]
    after = jnp.where(onward, two, one)[:reach]
    forward = jnp.concatenate([before, tokens, after])
    position = place * rows - reach + jnp.arange(forward.shape[0], dtype=jnp.int32)
    inside = (position >= 0) & (position < count * rows)
    backward = jnp.where(inside, LETTERS - forward, 0)[::-1]
    forward = jnp.where(inside, forward + 1, 0)
    lanes = []
    for strand in (forward, backward):
        for n in range(PARTS):
            lanes.append(strand[n * part_rows : n * part_rows + width])
    lanes += [jnp.zeros_like(lanes[0])] * (8 - WINDOWS)
    letters = jnp.stack(lanes)

    track_rows = up(part_rows, 16)
    hot_depth = 2 * LETTERS * up(short_len, 2)
    vmem = pl.BlockSpec(memory_space=pltpu.VMEM)
    hbm = pl.BlockSpec(memory_space=pltpu.HBM)
    partial = pl.pallas_call(
        functools.partial(kernel, (rows, short_len, taps, channels // filters, head_taps)),
        out_shape=jax.ShapeDtypeStruct((rows, outs), F32),
        in_specs=[vmem, hbm, hbm, hbm, hbm],
        out_specs=vmem,
        scratch_shapes=[
            pltpu.VMEM(nuc_table.shape, BF16),
            pltpu.VMEM(short_filter.shape, F32),
            pltpu.VMEM(mr_filter.shape, F32),
            pltpu.VMEM(head_weight.shape, BF16),
            pltpu.VMEM((WINDOWS * (window + 16), hot_depth), BF16),
            pltpu.VMEM((WINDOWS * track_rows, hot_depth), BF16),
            pltpu.VMEM((3, hot_depth, channels), BF16),
            pltpu.VMEM((filters, taps), F32),
            pltpu.VMEM((WINDOWS * track_rows, channels), BF16),
            pltpu.VMEM((STRANDS, part_rows + track_rows + 6, outs), F32),
            pltpu.SemaphoreType.DMA((4,)),
        ],
        compiler_params=pltpu.CompilerParams(vmem_limit_bytes=63 * 1024 * 1024),
        cost_estimate=pl.CostEstimate(
            flops=2 * 4 * 10**9, bytes_accessed=8 * 10**6, transcendentals=0
        ),
    )(letters, nuc_table, short_filter, mr_filter, head_weight)

    ring = [(i, (i + 1) % cores) for i in range(cores)]
    total, moving = partial, partial
    for _ in range(cores - 1):
        moving = lax.ppermute(moving, "ch", ring)
        total = total + moving
    return total.astype(BF16)


def solution(mesh):
    in_specs = (
        P(("groups", "seq")),
        P(None, None, "ch"),
        P(None, None, "ch"),
        P("ch", None),
        P(None, "ch", None),
    )
    out_specs = P(("groups", "seq"), None)
    return jax.shard_map(shards, mesh=mesh, in_specs=in_specs, out_specs=out_specs, check_vma=False)
```

time: 39 us -> 26.8 us (0.69)
  local copies, waits for them, and re-layouts: 5.51 us -> 0.98 us
  Pallas kernels: 19.7 us -> 15.4 us
  starting transfers between devices: 6.22 us -> 2.48 us
  other arithmetic: 1.52 us -> 2.41 us
  waiting for transfers between devices: 5.6 us -> 5.06 us
    unnamed x8 -> x0, local copies, waits for them, and re-layouts: 5.05 us -> none
    pallas_call x1, Pallas kernels: 19.7 us -> 15.4 us  [shards(): pl.pallas_call(functools.partial(kernel, (rows, short_len, taps, channels...]
    ppermute x2, starting transfers between devices: 6.15 us -> 2.41 us  [the longest x1 2.41 us: shards(): one = lax.ppermute(tokens, ('seq', 'ch'), ways)]
    convert_element_type x1, other arithmetic: 0.68 us -> 1.65 us  [shards(): return total.astype(BF16)]
    ppermute x2, waiting for transfers between devices: 4.08 us -> 3.32 us  [the longest x1 1.82 us: shards(): two = lax.ppermute(tokens, ('seq', 'ch'), [(b, a) for a, b in ways])]
    select_n x1 -> x2, other arithmetic: 0.08 us -> 0.76 us  [the longest x1 0.76 us: shards(): backward = jnp.where(inside, LETTERS - forward, 0)[::-1]]
    add x1 -> x0, other arithmetic: 0.68 us -> none  [shards(): coded = tokens + 1]
    another operation x6, local copies, waits for them, and re-layouts: 0.06 us -> 0.64 us  [shards(): letters = jnp.stack(lanes)]
  transfers between devices with their start and end apart: 3 -> 3, of which waited for: 2 -> 3; matrix products, arithmetic and copies ran while one was open for 0% -> 0% of each run, Pallas kernels for 0% -> 0%
where the time goes in v1:
time: 26.8 us; the launch traced here: 26.3 us
  Pallas kernels  15.4 us (57%)
  waiting for transfers between devices  5.06 us (19%)
  starting transfers between devices  2.48 us (9%)
  other arithmetic  2.41 us (9%)
  local copies, waits for them, and re-layouts  0.98 us (4%)
    pallas_call x1, Pallas kernels, shards(): pl.pallas_call(functools.partial(kernel, (rows, short_len, taps, channels...  15.4 us
    ppermute x1, starting transfers between devices, shards(): one = lax.ppermute(tokens, ('seq', 'ch'), ways)  2.41 us
    ppermute x1, waiting for transfers between devices, shards(): two = lax.ppermute(tokens, ('seq', 'ch'), [(b, a) for a, b in ways])  1.82 us
    ppermute x1, waiting for transfers between devices, shards(): moving = lax.ppermute(moving, 'ch', ring)  1.73 us
    convert_element_type x1, other arithmetic, shards(): return total.astype(BF16)  1.65 us
    ppermute x1, waiting for transfers between devices, shards(): one = lax.ppermute(tokens, ('seq', 'ch'), ways)  1.51 us
    select_n x1, other arithmetic, shards(): backward = jnp.where(inside, LETTERS - forward, 0)[::-1]  0.76 us
    another operation x6, local copies, waits for them, and re-layouts, shards(): letters = jnp.stack(lanes)  0.64 us
  transfers between devices with their start and end apart: 3, of which 3 were waited for; matrix products, arithmetic and copies ran while one was open for 0% of the time, Pallas kernels for 0%

profile of v1, /device:TPU:0, one launch (start us, length us, event | category | flops | bytes accessed | tf_op | source)
XLA Modules:
  0.0 26.3 jit_solution(17171210925084149145)
XLA Ops:
  0.0 2.4 %collective-permute-start = (s32[256]{0:T(256)}, s32[256]{0:T(256)S(1)}, u32[]{:S(2)}, u32[]{:S(2)}) collective-permute-start(s32[256]{0:T(256)} %param.5), channel_id=1, source_target_pairs={{0,3},{1,0},{2,1},{3,4},{4,7},{5,2},{6,5},{7,8},{8,11},{9,6},{10,9... | collective-permute-start | bytes 3080 | tf_op jit(solution)/shard_map/ppermute | solution.py:243
  2.4 0.0 collective-permute-start.1
  2.4 1.5 %collective-permute-done = s32[256]{0:T(256)S(1)} collective-permute-done((s32[256]{0:T(256)}, s32[256]{0:T(256)S(1)}, u32[]{:S(2)}, u32[]{:S(2)}) %collective-permute-start) | collective-permute-done | bytes 1056 | tf_op jit(solution)/shard_map/ppermute | solution.py:243
  3.9 1.8 %collective-permute-done.1 = s32[256]{0:T(256)S(1)} collective-permute-done((s32[256]{0:T(256)}, s32[256]{0:T(256)S(1)}, u32[]{:S(2)}, u32[]{:S(2)}) %collective-permute-start.1) | collective-permute-done | bytes 1056 | tf_op jit(solution)/shard_map/ppermute | solution.py:244
  5.7 0.1 slice.24
  5.8 0.8 %subtract_select_fusion = (s32[526]{0:T(1024)S(1)}, s32[526]{0:T(1024)S(1)}) fusion(s32[135]{0:T(256)S(1)} %bitcast.1, s32[256]{0:T(256)} %param.5, s32[135]{0:T(256)S(1)} %slice.24, s32[]{:T(128)S(6)} %sub.9), kind=kLoop, calls=%fused_computation.2 | loop fusion | flops 5260 | bytes 6316 | tf_op jit(solution)/shard_map/jit(_where)/select_n | solution.py:251
  6.6 0.1 fusion.3
  6.6 0.1 slice.31
  6.8 0.1 slice.29
  6.9 0.6 %stack.23.tok_ref = s32[8,384]{1,0:T(8,128)} concatenate(s32[1,384]{1,0:T(1,128)S(1)} %stack.18, s32[1,384]{1,0:T(1,128)S(1)} %stack.19, s32[1,384]{1,0:T(1,128)S(1)} %stack.20, s32[1,384]{1,0:T(1,128)S(1)} %stack.21, s32[4,384]{1,0:T(4,128)S(1)} %stack.22), dimensions={0} | concatenate | bytes 24576 | tf_op jit(solution)/shard_map/stack | solution.py:258
  7.5 15.4 %shard_map.55 = f32[256,256]{1,0:T(8,128)} custom-call(s32[8,384]{1,0:T(8,128)} %stack.23.tok_ref, bf16[3,4,2048]{2,1,0:T(4,128)(2,1)} %nuc_hbm.1, f32[3,7,2048]{2,1,0:T(8,128)} %sf_hbm.1, f32[128,128]{1,0:T(8,128)} %mr_hbm.1, bf16[5,2048,256]{2,1,0:T(8,128)(2,1)} %hw_hbm.1), custom_call_target="tpu_custom_call" | custom-call | flops 8000000000 | bytes 8000000 | tf_op jit(solution)/shard_map/pallas_call | solution.py:264
  22.9 0.1 collective-permute-start.2
  22.9 1.7 %collective-permute-done.2 = f32[256,256]{1,0:T(8,128)S(1)} collective-permute-done((f32[256,256]{1,0:T(8,128)}, f32[256,256]{1,0:T(8,128)S(1)}, u32[]{:S(2)}, u32[]{:S(2)}) %collective-permute-start.2) | collective-permute-done | bytes 262176 | tf_op jit(solution)/shard_map/ppermute | solution.py:291
  24.7 1.6 %add_convert_fusion = bf16[256,256]{1,0:T(8,128)(2,1)} fusion(f32[256,256]{1,0:T(8,128)} %shard_map.55, f32[256,256]{1,0:T(8,128)S(1)} %collective-permute-done.2), kind=kLoop, calls=%fused_computation | loop fusion | flops 131072 | bytes 655360 | tf_op jit(solution)/shard_map/convert_element_type | solution.py:293
  (6 shorter events, 0.0 us)
Async XLA Ops:
  0.0 3.9 %collective-permute-start = (s32[256]{0:T(256)}, s32[256]{0:T(256)S(1)}, u32[]{:S(2)}, u32[]{:S(2)}) collective-permute-start(s32[256]{0:T(256)} %param.5), channel_id=1, source_target_pairs={{0,3},{1,0},{2,1},{3,4},{4,7},{5,2},{6,5},{7,8},{8,11},{9,6},{10,9... | collective-permute-start | bytes 3080 | tf_op jit(solution)/shard_map/ppermute | solution.py:243
  2.4 3.3 %collective-permute-start.1 = (s32[256]{0:T(256)}, s32[256]{0:T(256)S(1)}, u32[]{:S(2)}, u32[]{:S(2)}) collective-permute-start(s32[256]{0:T(256)} %param.5), channel_id=1, source_target_pairs={{3,0},{0,1},{1,2},{4,3},{7,4},{2,5},{5,6},{8,7},{11,8},{6,9},{9,10... | collective-permute-start | bytes 3080 | tf_op jit(solution)/shard_map/ppermute | solution.py:244
  22.9 1.8 %collective-permute-start.2 = (f32[256,256]{1,0:T(8,128)}, f32[256,256]{1,0:T(8,128)S(1)}, u32[]{:S(2)}, u32[]{:S(2)}) collective-permute-start(f32[256,256]{1,0:T(8,128)} %shard_map.55), channel_id=1, source_target_pairs={{0,1},{1,0},{2,3},{3,2},{4,5},{5,4},{6,7},{7,6},{8,9},{9,8},{10,11... | collective-permute-start | bytes 786440 | tf_op jit(solution)/shard_map/ppermute | solution.py:291

commit v2 on v1

v2 whole, which is shorter than its diff:
```python
import functools

import jax
import jax.numpy as jnp
from jax import lax
from jax.experimental import pallas as pl
from jax.experimental.pallas import tpu as pltpu
from jax.sharding import PartitionSpec as P

LANES = 128
HALF = 64
WIDE = 256
SUB = 8
PACK = 16
LETTERS = 4
STRANDS = 2
PARTS = 2
F32 = jnp.float32
BF16 = jnp.bfloat16
MIB = 1024 * 1024


def up(value, step):
    return -(-value // step) * step


def iota(shape, dim):
    return lax.broadcasted_iota(jnp.int32, shape, dim)


def dot(a, b):
    return jnp.dot(a, b, preferred_element_type=F32)


def ones_where(mask):
    return mask.astype(F32).astype(BF16)


class Plan:
    def __init__(self, rows, short_len, taps, head_taps):
        self.rows, self.short_len, self.taps, self.head_taps = rows, short_len, taps, head_taps
        self.rim = (head_taps - 1) // 2
        self.part = rows // PARTS
        self.window = 2 * taps
        self.offset = self.window - self.part - 2 * self.rim
        self.missing = taps - 1 - self.offset
        self.mix_rows = up(self.part + 2 * self.rim, PACK)
        self.track_rows = (PARTS - 1) * self.part + self.mix_rows
        self.hot_rows = PACK + (PARTS - 1) * self.part + self.window
        self.lead = PACK + self.offset + self.rim + short_len - 1
        self.query_lead = PACK + self.offset
        self.width = up(self.query_lead + self.track_rows + short_len, LANES)
        self.depth = 2 * LETTERS * up(short_len, 2)


def build_weights(plan, nuc_ref, sf_ref, wn_ref):
    row = iota((2 * LETTERS, WIDE), 0)
    first = row < LETTERS
    short_len = plan.short_len

    def step(v, carry):
        lanes = pl.ds(pl.multiple_of(v * WIDE, WIDE), WIDE)
        for m in range(3):
            nuc = nuc_ref[m, :, lanes].astype(F32)
            nuc = jnp.concatenate([nuc, nuc], axis=0)
            taps = sf_ref[m, :, lanes]
            pieces = []
            for lag in range(0, short_len, 2):
                a = jnp.broadcast_to(taps[lag : lag + 1], row.shape)
                if lag + 1 < short_len:
                    b = jnp.broadcast_to(taps[lag + 1 : lag + 2], row.shape)
                else:
                    b = jnp.zeros(row.shape, F32)
                pieces.append(jnp.where(first, a, b) * nuc)
            product = jnp.concatenate(pieces, axis=0)
            high = product.astype(BF16)
            low = (product - high.astype(F32)).astype(BF16)
            wn_ref[m, :, lanes] = jnp.concatenate([high, low], axis=0)
        return carry

    lax.fori_loop(0, nuc_ref.shape[2] // WIDE, step, 0)


def build_mixers(plan, mr_ref, fr_ref, mixer_ref):
    taps, rows = plan.taps, plan.mix_rows
    total = iota((taps, taps), 0) + iota((taps, taps), 1)
    turn = (total == plan.offset) | (total == plan.offset + taps)
    fr_ref[...] = dot(mr_ref[...].astype(BF16), ones_where(turn))
    gap = iota((rows, taps), 0) - iota((rows, taps), 1)
    near_mask = (gap <= plan.missing) & (gap >= -plan.offset)
    far_mask = gap > plan.missing
    filters = mr_ref.shape[0]

    def step(b, carry):
        block = fr_ref[pl.ds(pl.multiple_of(b * SUB, SUB), SUB), :]
        for g in range(SUB):
            wide = jnp.broadcast_to(block[g : g + 1], (taps, taps))
            turned = pltpu.roll(wide, 0, 1, stride=1, stride_axis=0)
            turned = jnp.concatenate([turned, turned[: rows - taps]], axis=0)
            zero = jnp.zeros_like(turned)
            at = pl.ds(pl.multiple_of((b * SUB + g) * rows, rows), rows)
            mixer_ref[at, :taps] = jnp.where(near_mask, turned, zero).astype(BF16)
            mixer_ref[at, taps:] = jnp.where(far_mask, turned, zero).astype(BF16)
        return carry

    lax.fori_loop(0, filters // SUB, step, 0)


def build_edges(plan, mr_ref, edge_ref):
    filters, taps = mr_ref.shape
    channels = edge_ref.shape[1]
    rows = edge_ref.shape[0]
    row, tap = iota((rows, taps), 0), iota((rows, taps), 1)
    wanted = tap == row % SUB + plan.offset + 1 + row // SUB
    picked = lax.dot_general(
        ones_where(wanted), mr_ref[...].astype(BF16), (((1,), (1,)), ((), ())), preferred_element_type=F32
    ).astype(BF16)
    width = channels // filters

    def step(v, carry):
        shape = (filters, WIDE)
        spread = ones_where(iota(shape, 0) == (iota(shape, 1) + v * WIDE) // width)
        edge_ref[:, pl.ds(pl.multiple_of(v * WIDE, WIDE), WIDE)] = dot(picked, spread)
        return carry

    lax.fori_loop(0, channels // WIDE, step, 0)


def prepare(
    plan, own_hbm, nuc_hbm, sf_hbm, mr_hbm, own_ref, wn_ref, mixer_ref, edge_ref,
    nuc_ref, sf_ref, mr_ref, fr_ref, sems,
):
    pairs = [(mr_hbm, mr_ref), (nuc_hbm, nuc_ref), (sf_hbm, sf_ref), (own_hbm, own_ref)]
    copies = [pltpu.make_async_copy(a, b, sems.at[i]) for i, (a, b) in enumerate(pairs)]
    for copy in copies:
        copy.start()
    copies[0].wait()
    build_mixers(plan, mr_ref, fr_ref, mixer_ref)
    build_edges(plan, mr_ref, edge_ref)
    for copy in copies[1:]:
        copy.wait()
    build_weights(plan, nuc_ref, sf_ref, wn_ref)


def coded_letters(plan, count, one_ref, own_ref, two_ref):
    place = lax.axis_index("seq")
    onward = lax.rem(place + lax.axis_index("ch"), 2) == 0
    one, two = one_ref[...], two_ref[...]
    before = jnp.where(onward, one, two) + 1
    after = jnp.where(onward, two, one) + 1
    before = jnp.where(place > 0, before, 0)
    after = jnp.where(place < count - 1, after, 0)
    around = jnp.concatenate([before, own_ref[...] + 1, after], axis=1)
    blocks = around.shape[1] // LANES
    pieces = [around[:, i * LANES : (i + 1) * LANES] for i in range(blocks)]
    pieces += [jnp.zeros_like(pieces[0])] * (up(blocks, SUB) - blocks)
    flip = ones_where(iota((LANES, LANES), 0) + iota((LANES, LANES), 1) == LANES - 1)
    turned = dot(jnp.concatenate(pieces, axis=0).astype(F32).astype(BF16), flip).astype(jnp.int32)
    back = jnp.concatenate([turned[i : i + 1] for i in reversed(range(blocks))], axis=1)
    back = jnp.where(back > 0, LETTERS + 1 - back, 0)
    rest = jnp.zeros((SUB - STRANDS, around.shape[1]), jnp.int32)
    return jnp.concatenate([around, back, rest], axis=0)


def build_onehot(plan, tok, hot_ref, query_ref):
    width = tok.shape[1]
    hot_lanes, query_lanes = up(plan.hot_rows, LANES), up(plan.track_rows, LANES)
    lags = []
    for lag in range(plan.short_len):
        lead = plan.rows - plan.lead + plan.short_len - 1 - lag
        a = pltpu.roll(tok, (width - lead) % width, 1)[:, :hot_lanes]
        b = pltpu.roll(tok, (width - lead - plan.query_lead) % width, 1)[:, :query_lanes]
        lags.append(jnp.concatenate([a, b], axis=1))
    own = lags[0] > 0
    zero = jnp.zeros_like(lags[0])
    lags = [jnp.where(own, lag, zero) for lag in lags]
    if len(lags) % 2:
        lags.append(zero)
    row = iota((2 * LETTERS, zero.shape[1]), 0)
    first = row < LETTERS
    letter = jnp.where(first, row, row - LETTERS) + 1
    for s in range(STRANDS):
        pieces = []
        for lag in range(0, len(lags), 2):
            a = jnp.broadcast_to(lags[lag][s : s + 1], row.shape)
            b = jnp.broadcast_to(lags[lag + 1][s : s + 1], row.shape)
            pieces.append((jnp.where(first, a, b) == letter).astype(F32))
        hot = jnp.concatenate(pieces + pieces, axis=0).T.astype(BF16)
        hot_ref[s] = hot[: plan.hot_rows]
        query_ref[s] = hot[hot_lanes : hot_lanes + plan.track_rows]


def kernel(
    plan, count, one_ref, own_ref, two_ref, wn_ref, mixer_ref, edge_ref, hw_hbm, out_ref,
    hw_ref, hot_ref, query_ref, track_ref, score_ref, sem,
):
    channels = wn_ref.shape[2]
    part, window, mix_rows = plan.part, plan.window, plan.mix_rows
    group_width = channels * mix_rows // mixer_ref.shape[0]
    tile_groups = HALF // group_width
    tile_rows = tile_groups * mix_rows

    fetch = pltpu.make_async_copy(hw_hbm, hw_ref, sem)
    fetch.start()
    tok = coded_letters(plan, count, one_ref, own_ref, two_ref)
    build_onehot(plan, tok, hot_ref, query_ref)

    lane_group = (iota((mix_rows, WIDE), 1) % HALF) // group_width
    low_half = iota((window, LANES), 1) < HALF
    low_mix = low_half[:mix_rows]

    def step(v, carry):
        lanes = pl.ds(pl.multiple_of(v * WIDE, WIDE), WIDE)
        gated, query = [], []
        for s in range(STRANDS):
            gated.append(dot(hot_ref[s], wn_ref[1, :, lanes]) * dot(hot_ref[s], wn_ref[2, :, lanes]))
            query.append(dot(query_ref[s], wn_ref[0, :, lanes]))
        for j in range(WIDE // LANES):
            some = slice(j * LANES, (j + 1) * LANES)
            to = pl.ds(pl.multiple_of(v * WIDE + j * LANES, LANES), LANES)
            lower, upper = [], []
            for s in range(STRANDS):
                a = gated[s][PACK : PACK + window, some]
                b = pltpu.roll(gated[s][PACK + part : PACK + part + window, some], HALF, 1)
                lower.append(jnp.where(low_half, a, b))
                upper.append(jnp.where(low_half, b, a))
            mixed = []
            for h, halves in enumerate((lower, upper)):
                data = jnp.concatenate(halves, axis=1).astype(BF16)
                tile = v * (WIDE // HALF) + 2 * j + h
                mixers = mixer_ref[pl.ds(pl.multiple_of(tile * tile_rows, tile_rows), tile_rows), :]
                pieces = dot(mixers, data)
                chosen = pieces[:mix_rows]
                for g in range(1, tile_groups):
                    chosen = jnp.where(lane_group == g, pieces[g * mix_rows : (g + 1) * mix_rows], chosen)
                mixed.append(chosen)
            for s in range(STRANDS):
                a, b = (m[:, s * LANES : (s + 1) * LANES] for m in mixed)
                both = [jnp.where(low_mix, a, b), pltpu.roll(jnp.where(low_mix, b, a), HALF, 1)]
                for p in range(PARTS):
                    fix = both[p][:SUB]
                    for d in range(plan.missing):
                        at = PACK + p * part - 1 - d
                        fix = fix + edge_ref[d * SUB : (d + 1) * SUB, to] * gated[s][at : at + 1, some]
                    length = part if p < PARTS - 1 else mix_rows
                    whole = jnp.concatenate([fix, both[p][SUB:length]], axis=0)
                    own = query[s][p * part : p * part + length, some]
                    at = s * plan.track_rows + p * part
                    track_ref[at : at + length, to] = (own * whole).astype(BF16)
        return carry

    lax.fori_loop(0, channels // WIDE, step, 0)

    fetch.wait()
    totals = [None, None]
    for k in range(plan.head_taps):
        score = dot(track_ref[...], hw_ref[k])
        for s in range(STRANDS):
            score_ref[s] = score[s * plan.track_rows : (s + 1) * plan.track_rows]
            shifted = score_ref[s, k : k + plan.rows]
            totals[s] = shifted if k == 0 else totals[s] + shifted
    forward, backward = totals
    flip = ones_where(iota((plan.rows, plan.rows), 0) + iota((plan.rows, plan.rows), 1) == plan.rows - 1)
    for _ in range(3):
        high = backward.astype(BF16)
        forward = forward + dot(flip, high)
        backward = backward - high.astype(F32)
    out_ref[...] = forward


def neighbour_ways(count, cores):
    ways = []
    for i in range(count):
        for c in range(cores):
            step = 1 if (i + c) % 2 == 0 else -1
            there = (i + step, c ^ 1) if 0 <= i + step < count else (i, c ^ 1)
            ways.append((i * cores + c, there[0] * cores + there[1]))
    return ways


def stay(array):
    return pltpu.with_memory_space_constraint(array, pltpu.HBM)


def shards(tokens, nuc_table, short_filter, mr_filter, head_weight):
    _, short_len, channels = short_filter.shape
    filters, taps = mr_filter.shape
    head_taps, _, outs = head_weight.shape
    plan = Plan(tokens.shape[0], short_len, taps, head_taps)
    vmem = pl.BlockSpec(memory_space=pltpu.VMEM)
    hbm = pl.BlockSpec(memory_space=pl.ANY)

    own = tokens.reshape(1, plan.rows)
    own_here, weights, mixers, edges = pl.pallas_call(
        functools.partial(prepare, plan),
        out_shape=(
            jax.ShapeDtypeStruct(own.shape, own.dtype),
            jax.ShapeDtypeStruct((3, plan.depth, channels), BF16),
            jax.ShapeDtypeStruct((filters * plan.mix_rows, plan.window), BF16),
            jax.ShapeDtypeStruct((up(plan.missing, 1) * SUB, channels), F32),
        ),
        in_specs=[hbm] * 4,
        out_specs=(vmem,) * 4,
        scratch_shapes=[
            pltpu.VMEM(nuc_table.shape, BF16),
            pltpu.VMEM(short_filter.shape, F32),
            pltpu.VMEM(mr_filter.shape, F32),
            pltpu.VMEM(mr_filter.shape, F32),
            pltpu.SemaphoreType.DMA((4,)),
        ],
        compiler_params=pltpu.CompilerParams(vmem_limit_bytes=16 * MIB),
        cost_estimate=pl.CostEstimate(flops=10**8, bytes_accessed=10**7, transcendentals=0),
        name="prepare",
    )(*(stay(a) for a in (own, nuc_table, short_filter, mr_filter)))

    count, cores = lax.axis_size("seq"), lax.axis_size("ch")
    ways = neighbour_ways(count, cores)
    one = lax.ppermute(own, ("seq", "ch"), ways)
    two = lax.ppermute(own, ("seq", "ch"), [(b, a) for a, b in ways])

    partial = pl.pallas_call(
        functools.partial(kernel, plan, count),
        out_shape=jax.ShapeDtypeStruct((plan.rows, outs), F32),
        in_specs=[vmem] * 6 + [hbm],
        out_specs=vmem,
        scratch_shapes=[
            pltpu.VMEM(head_weight.shape, BF16),
            pltpu.VMEM((STRANDS, plan.hot_rows, plan.depth), BF16),
            pltpu.VMEM((STRANDS, plan.track_rows, plan.depth), BF16),
            pltpu.VMEM((STRANDS * plan.track_rows, channels), BF16),
            pltpu.VMEM((STRANDS, plan.track_rows, outs), F32),
            pltpu.SemaphoreType.DMA,
        ],
        compiler_params=pltpu.CompilerParams(vmem_limit_bytes=24 * MIB),
        cost_estimate=pl.CostEstimate(flops=8 * 10**9, bytes_accessed=10**7, transcendentals=0),
        name="annotate",
    )(one, own_here, two, weights, mixers, edges, stay(head_weight))

    ring = [(i, (i + 1) % cores) for i in range(cores)]
    total, moving = partial, partial
    for _ in range(cores - 1):
        moving = lax.ppermute(moving, "ch", ring)
        total = total + moving
    return total.astype(BF16)


def solution(mesh):
    in_specs = (
        P(("groups", "seq")),
        P(None, None, "ch"),
        P(None, None, "ch"),
        P("ch", None),
        P(None, "ch", None),
    )
    out_specs = P(("groups", "seq"), None)
    return jax.shard_map(shards, mesh=mesh, in_specs=in_specs, out_specs=out_specs, check_vma=False)
```

time: 26.8 us -> 22.9 us (0.85); the launches traced: 26.3 us -> 22.8 us
  waiting for transfers between devices: 5.06 us -> 1.17 us
  Pallas kernels: 15.4 us -> 17.8 us
  other arithmetic: 2.41 us -> 0.68 us
  local copies, waits for them, and re-layouts: 0.98 us -> 0 us
  starting transfers between devices: 2.48 us -> 3.15 us
    ppermute x2, waiting for transfers between devices: 3.32 us -> 0.01 us  [the longest x1 0.01 us: shards(): two = lax.ppermute(own, ('seq', 'ch'), [(b, a) for a, b in ways])]
    pallas_call x1 -> x2, Pallas kernels: 15.4 us -> 17.8 us  [the longest x1 12.2 us: shards(): pl.pallas_call(functools.partial(kernel, plan, count), out_shape=jax.Shap...]
    convert_element_type x1, other arithmetic: 1.65 us -> 0.68 us  [shards(): return total.astype(BF16)]
    select_n x2 -> x0, other arithmetic: 0.76 us -> none  [the longest x1 0.76 us: shards(): backward = jnp.where(inside, LETTERS - forward, 0)[::-1]]
    ppermute x1, starting transfers between devices: 0.07 us -> 0.74 us  [shards(): moving = lax.ppermute(moving, 'ch', ring)]
    another operation x6 -> x0, local copies, waits for them, and re-layouts: 0.64 us -> none  [shards(): letters = jnp.stack(lanes)]
    ppermute x1, waiting for transfers between devices: 1.73 us -> 1.16 us  [shards(): moving = lax.ppermute(moving, 'ch', ring)]
    slice x4 -> x0, local copies, waits for them, and re-layouts: 0.34 us -> none  [the longest x3 0.27 us: shards(): lanes.append(strand[n * part_rows:n * part_rows + width])]
  transfers between devices with their start and end apart: 3 -> 3, of which waited for: 3 -> 1; matrix products, arithmetic and copies ran while one was open for 0% -> 0% of each run, Pallas kernels for 0% -> 25%
where the time goes in v2:
time: 22.9 us; the launch traced here: 22.8 us
  Pallas kernels  17.8 us (78%)
  starting transfers between devices  3.15 us (14%)
  waiting for transfers between devices  1.17 us (5%)
  other arithmetic  0.68 us (3%)
    pallas_call x1, Pallas kernels, shards(): pl.pallas_call(functools.partial(kernel, plan, count), out_shape=jax.Shap...  12.2 us
    pallas_call x1, Pallas kernels, shards(): pl.pallas_call(functools.partial(prepare, plan), out_shape=(jax.ShapeDtyp...  5.59 us
    ppermute x1, starting transfers between devices, shards(): one = lax.ppermute(own, ('seq', 'ch'), ways)  1.92 us
    ppermute x1, waiting for transfers between devices, shards(): moving = lax.ppermute(moving, 'ch', ring)  1.16 us
    ppermute x1, starting transfers between devices, shards(): moving = lax.ppermute(moving, 'ch', ring)  0.74 us
    convert_element_type x1, other arithmetic, shards(): return total.astype(BF16)  0.68 us
    ppermute x1, starting transfers between devices, shards(): two = lax.ppermute(own, ('seq', 'ch'), [(b, a) for a, b in ways])  0.49 us
  transfers between devices with their start and end apart: 3, of which 1 were waited for; matrix products, arithmetic and copies ran while one was open for 0% of the time, Pallas kernels for 25%

profile of v2, /device:TPU:0, one launch (start us, length us, event | category | flops | bytes accessed | tf_op | source)
XLA Modules:
  0.0 22.8 jit_solution(2397806874488977155)
XLA Ops:
  0.0 0.5 %collective-permute-start.1 = (s32[1,256]{1,0:T(1,128)}, s32[1,256]{1,0:T(1,128)S(1)}, u32[]{:S(2)}, u32[]{:S(2)}) collective-permute-start(s32[1,256]{1,0:T(1,128)} %bitcast.1), channel_id=1, source_target_pairs={{3,0},{0,1},{1,2},{4,3},{7,4},{2,5},{5,6},{8,7},{11,8},{6,9},{9,10... | collective-permute-start | bytes 3080 | tf_op jit(solution)/shard_map/ppermute | solution.py:319
  0.5 1.9 %collective-permute-start = (s32[1,256]{1,0:T(1,128)}, s32[1,256]{1,0:T(1,128)S(1)}, u32[]{:S(2)}, u32[]{:S(2)}) collective-permute-start(s32[1,256]{1,0:T(1,128)} %bitcast.2), channel_id=1, source_target_pairs={{0,3},{1,0},{2,1},{3,4},{4,7},{5,2},{6,5},{7,8},{8,11},{9,6},{10,9... | collective-permute-start | bytes 3080 | tf_op jit(solution)/shard_map/ppermute | solution.py:318
  2.4 5.6 %prepare.1 = (s32[1,256]{1,0:T(1,128)S(1)}, bf16[3,64,2048]{2,1,0:T(8,128)(2,1)S(1)}, bf16[18432,256]{1,0:T(8,128)(2,1)S(1)}, f32[24,2048]{1,0:T(8,128)S(1)}) custom-call(s32[1,256]{1,0:T(1,128)} %bitcast.3, bf16[3,4,2048]{2,1,0:T(4,128)(2,1)} %nuc_hbm.1, f32[3,7,2048]{2,1,0:T(8,128)} %sf_hbm.1, f32[128,128]{1,0:T(8,128)} %mr_hbm.1), custom_call_target="tpu_custom_call" | custom-call | flops 100000000 | bytes 10000000 | tf_op jit(solution)/shard_map/prepare/pallas_call | solution.py:294
  8.0 0.0 collective-permute-done.1.two_ref
  8.0 0.0 collective-permute-done.one_ref
  8.0 12.2 %annotate.1 = f32[256,256]{1,0:T(8,128)S(1)} custom-call(s32[1,256]{1,0:T(1,128)S(1)} %collective-permute-done.one_ref, s32[1,256]{1,0:T(1,128)S(1)} %get-tuple-element.9.own_ref, s32[1,256]{1,0:T(1,128)S(1)} %collective-permute-done.1.two_ref, bf16[3,64,2048]{2,1,0:T(8,128)(2,1)S(1)} %get-tuple-element.10.wn_ref, ...), custom_call_target="tpu_custom_call" | custom-call | flops 8000000000 | bytes 10000000 | tf_op jit(solution)/shard_map/annotate/pallas_call | solution.py:321
  20.2 0.7 %collective-permute-start.2 = (f32[256,256]{1,0:T(8,128)S(1)}, f32[256,256]{1,0:T(8,128)S(1)}, u32[]{:S(2)}, u32[]{:S(2)}) collective-permute-start(f32[256,256]{1,0:T(8,128)S(1)} %annotate.1), channel_id=1, source_target_pairs={{0,1},{1,0},{2,3},{3,2},{4,5},{5,4},{6,7},{7,6},{8,9},{9,8},{10,11... | collective-permute-start | bytes 786440 | tf_op jit(solution)/shard_map/ppermute | solution.py:342
  20.9 1.2 %collective-permute-done.2 = f32[256,256]{1,0:T(8,128)S(1)} collective-permute-done((f32[256,256]{1,0:T(8,128)S(1)}, f32[256,256]{1,0:T(8,128)S(1)}, u32[]{:S(2)}, u32[]{:S(2)}) %collective-permute-start.2) | collective-permute-done | bytes 262176 | tf_op jit(solution)/shard_map/ppermute | solution.py:342
  22.1 0.7 %add_convert_fusion = bf16[256,256]{1,0:T(8,128)(2,1)} fusion(f32[256,256]{1,0:T(8,128)S(1)} %annotate.1, f32[256,256]{1,0:T(8,128)S(1)} %collective-permute-done.2), kind=kLoop, calls=%fused_computation | loop fusion | flops 131072 | bytes 655360 | tf_op jit(solution)/shard_map/convert_element_type | solution.py:344
Async XLA Ops:
  0.0 8.0 %collective-permute-start.1 = (s32[1,256]{1,0:T(1,128)}, s32[1,256]{1,0:T(1,128)S(1)}, u32[]{:S(2)}, u32[]{:S(2)}) collective-permute-start(s32[1,256]{1,0:T(1,128)} %bitcast.1), channel_id=1, source_target_pairs={{3,0},{0,1},{1,2},{4,3},{7,4},{2,5},{5,6},{8,7},{11,8},{6,9},{9,10... | collective-permute-start | bytes 3080 | tf_op jit(solution)/shard_map/ppermute | solution.py:319
  0.5 7.5 %collective-permute-start = (s32[1,256]{1,0:T(1,128)}, s32[1,256]{1,0:T(1,128)S(1)}, u32[]{:S(2)}, u32[]{:S(2)}) collective-permute-start(s32[1,256]{1,0:T(1,128)} %bitcast.2), channel_id=1, source_target_pairs={{0,3},{1,0},{2,1},{3,4},{4,7},{5,2},{6,5},{7,8},{8,11},{9,6},{10,9... | collective-permute-start | bytes 3080 | tf_op jit(solution)/shard_map/ppermute | solution.py:318
  20.2 1.9 %collective-permute-start.2 = (f32[256,256]{1,0:T(8,128)S(1)}, f32[256,256]{1,0:T(8,128)S(1)}, u32[]{:S(2)}, u32[]{:S(2)}) collective-permute-start(f32[256,256]{1,0:T(8,128)S(1)} %annotate.1), channel_id=1, source_target_pairs={{0,1},{1,0},{2,3},{3,2},{4,5},{5,4},{6,7},{7,6},{8,9},{9,8},{10,11... | collective-permute-start | bytes 786440 | tf_op jit(solution)/shard_map/ppermute | solution.py:342

commit v3 on v2

--- a/solution.py
+++ b/solution.py
@@ -87,20 +87,19 @@
     turn = (total == plan.offset) | (total == plan.offset + taps)
     fr_ref[...] = dot(mr_ref[...].astype(BF16), ones_where(turn))
     gap = iota((rows, taps), 0) - iota((rows, taps), 1)
-    near_mask = (gap <= plan.missing) & (gap >= -plan.offset)
-    far_mask = gap > plan.missing
+    near_mask = ones_where((gap <= plan.missing) & (gap >= -plan.offset))
+    far_mask = ones_where(gap > plan.missing)
     filters = mr_ref.shape[0]
 
     def step(b, carry):
         block = fr_ref[pl.ds(pl.multiple_of(b * SUB, SUB), SUB), :]
         for g in range(SUB):
             wide = jnp.broadcast_to(block[g : g + 1], (taps, taps))
-            turned = pltpu.roll(wide, 0, 1, stride=1, stride_axis=0)
+            turned = pltpu.roll(wide, 0, 1, stride=1, stride_axis=0).astype(BF16)
             turned = jnp.concatenate([turned, turned[: rows - taps]], axis=0)
-            zero = jnp.zeros_like(turned)
             at = pl.ds(pl.multiple_of((b * SUB + g) * rows, rows), rows)
-            mixer_ref[at, :taps] = jnp.where(near_mask, turned, zero).astype(BF16)
-            mixer_ref[at, taps:] = jnp.where(far_mask, turned, zero).astype(BF16)
+            mixer_ref[at, :taps] = turned * near_mask
+            mixer_ref[at, taps:] = turned * far_mask
         return carry
 
     lax.fori_loop(0, filters // SUB, step, 0)
@@ -192,7 +191,7 @@
 
 def kernel(
     plan, count, one_ref, own_ref, two_ref, wn_ref, mixer_ref, edge_ref, hw_hbm, out_ref,
-    hw_ref, hot_ref, query_ref, track_ref, score_ref, sem,
+    hw_ref, hot_ref, query_ref, data_now, edge_now, query_now, track_ref, score_ref, sem,
 ):
     channels = wn_ref.shape[2]
     part, window, mix_rows = plan.part, plan.window, plan.mix_rows
@@ -209,47 +208,61 @@
     low_half = iota((window, LANES), 1) < HALF
     low_mix = low_half[:mix_rows]
 
-    def step(v, carry):
-        lanes = pl.ds(pl.multiple_of(v * WIDE, WIDE), WIDE)
-        gated, query = [], []
-        for s in range(STRANDS):
-            gated.append(dot(hot_ref[s], wn_ref[1, :, lanes]) * dot(hot_ref[s], wn_ref[2, :, lanes]))
-            query.append(dot(query_ref[s], wn_ref[0, :, lanes]))
+    steps = channels // WIDE
+
+    def gate(v, s):
+        lanes = pl.ds(v * WIDE, WIDE)
+        slot = v % 2
+        hot = hot_ref[s]
+        gated = dot(hot, wn_ref[1, :, lanes]) * dot(hot, wn_ref[2, :, lanes])
+        query_now[slot, s] = dot(query_ref[s], wn_ref[0, :, lanes])
+        for p in range(PARTS):
+            at = PACK + p * part
+            edge_now[slot, s, p] = gated[at - SUB : at]
         for j in range(WIDE // LANES):
             some = slice(j * LANES, (j + 1) * LANES)
-            to = pl.ds(pl.multiple_of(v * WIDE + j * LANES, LANES), LANES)
-            lower, upper = [], []
-            for s in range(STRANDS):
-                a = gated[s][PACK : PACK + window, some]
-                b = pltpu.roll(gated[s][PACK + part : PACK + part + window, some], HALF, 1)
-                lower.append(jnp.where(low_half, a, b))
-                upper.append(jnp.where(low_half, b, a))
-            mixed = []
-            for h, halves in enumerate((lower, upper)):
-                data = jnp.concatenate(halves, axis=1).astype(BF16)
-                tile = v * (WIDE // HALF) + 2 * j + h
-                mixers = mixer_ref[pl.ds(pl.multiple_of(tile * tile_rows, tile_rows), tile_rows), :]
-                pieces = dot(mixers, data)
-                chosen = pieces[:mix_rows]
-                for g in range(1, tile_groups):
-                    chosen = jnp.where(lane_group == g, pieces[g * mix_rows : (g + 1) * mix_rows], chosen)
-                mixed.append(chosen)
-            for s in range(STRANDS):
-                a, b = (m[:, s * LANES : (s + 1) * LANES] for m in mixed)
-                both = [jnp.where(low_mix, a, b), pltpu.roll(jnp.where(low_mix, b, a), HALF, 1)]
-                for p in range(PARTS):
-                    fix = both[p][:SUB]
-                    for d in range(plan.missing):
-                        at = PACK + p * part - 1 - d
-                        fix = fix + edge_ref[d * SUB : (d + 1) * SUB, to] * gated[s][at : at + 1, some]
-                    length = part if p < PARTS - 1 else mix_rows
-                    whole = jnp.concatenate([fix, both[p][SUB:length]], axis=0)
-                    own = query[s][p * part : p * part + length, some]
-                    at = s * plan.track_rows + p * part
-                    track_ref[at : at + length, to] = (own * whole).astype(BF16)
-        return carry
-
-    lax.fori_loop(0, channels // WIDE, step, 0)
+            a = gated[PACK : PACK + window, some]
+            b = pltpu.roll(gated[PACK + part : PACK + part + window, some], HALF, 1)
+            to = slice(s * LANES, (s + 1) * LANES)
+            data_now[slot, 2 * j, :, to] = jnp.where(low_half, a, b).astype(BF16)
+            data_now[slot, 2 * j + 1, :, to] = jnp.where(low_half, b, a).astype(BF16)
+
+    def mix(v, j):
+        slot = v % 2
+        some = slice(j * LANES, (j + 1) * LANES)
+        to = pl.ds(v * WIDE + j * LANES, LANES)
+        mixed = []
+        for h in range(2):
+            tile = v * (WIDE // HALF) + 2 * j + h
+            mixers = mixer_ref[pl.ds(tile * tile_rows, tile_rows), :]
+            data = data_now[slot, 2 * j + h]
+            middle = tile_rows // 2
+            pieces = jnp.concatenate([dot(mixers[:middle], data), dot(mixers[middle:], data)], axis=0)
+            chosen = pieces[:mix_rows]
+            for g in range(1, tile_groups):
+                chosen = jnp.where(lane_group == g, pieces[g * mix_rows : (g + 1) * mix_rows], chosen)
+            mixed.append(chosen)
+        for s in range(STRANDS):
+            a, b = (m[:, s * LANES : (s + 1) * LANES] for m in mixed)
+            both = [jnp.where(low_mix, a, b), pltpu.roll(jnp.where(low_mix, b, a), HALF, 1)]
+            for p in range(PARTS):
+                fix = both[p][:SUB]
+                for d in range(plan.missing):
+                    base = edge_now[slot, s, p, SUB - 1 - d : SUB - d, some]
+                    fix = fix + edge_ref[d * SUB : (d + 1) * SUB, to] * base
+                length = part if p < PARTS - 1 else mix_rows
+                whole = jnp.concatenate([fix, both[p][SUB:length]], axis=0)
+                own = query_now[slot, s, p * part : p * part + length, some]
+                at = s * plan.track_rows + p * part
+                track_ref[at : at + length, to] = (own * whole).astype(BF16)
+
+    for s in range(STRANDS):
+        gate(0, s)
+    for v in range(steps):
+        for i in range(2):
+            if v + 1 < steps:
+                gate(v + 1, i)
+            mix(v, i)
 
     fetch.wait()
     totals = [None, None]
@@ -327,6 +340,9 @@
             pltpu.VMEM(head_weight.shape, BF16),
             pltpu.VMEM((STRANDS, plan.hot_rows, plan.depth), BF16),
             pltpu.VMEM((STRANDS, plan.track_rows, plan.depth), BF16),
+            pltpu.VMEM((2, WIDE // HALF, plan.window, WIDE), BF16),
+            pltpu.VMEM((2, STRANDS, PARTS, SUB, WIDE), F32),
+            pltpu.VMEM((2, STRANDS, plan.track_rows, WIDE), F32),
             pltpu.VMEM((STRANDS * plan.track_rows, channels), BF16),
             pltpu.VMEM((STRANDS, plan.track_rows, outs), F32),
             pltpu.SemaphoreType.DMA,

time: 22.9 us -> 21.9 us (0.956)
  Pallas kernels: 17.8 us -> 16.8 us
    pallas_call x1, Pallas kernels: 12.2 us -> 11.5 us  [shards(): pl.pallas_call(functools.partial(kernel, plan, count), out_shape=jax.Shap...]
    pallas_call x1, Pallas kernels: 5.59 us -> 5.27 us  [shards(): pl.pallas_call(functools.partial(prepare, plan), out_shape=(jax.ShapeDtyp...]
  transfers between devices with their start and end apart: 3 -> 3, of which waited for: 1 -> 1; matrix products, arithmetic and copies ran while one was open for 0% -> 0% of each run, Pallas kernels for 25% -> 24%
where the time goes in v3:
time: 21.9 us; the launch traced here: 21.8 us
  Pallas kernels  16.8 us (77%)
  starting transfers between devices  3.15 us (14%)
  waiting for transfers between devices  1.17 us (5%)
  other arithmetic  0.68 us (3%)
    pallas_call x1, Pallas kernels, shards(): pl.pallas_call(functools.partial(kernel, plan, count), out_shape=jax.Shap...  11.5 us
    pallas_call x1, Pallas kernels, shards(): pl.pallas_call(functools.partial(prepare, plan), out_shape=(jax.ShapeDtyp...  5.27 us
    ppermute x1, starting transfers between devices, shards(): one = lax.ppermute(own, ('seq', 'ch'), ways)  1.92 us
    ppermute x1, waiting for transfers between devices, shards(): moving = lax.ppermute(moving, 'ch', ring)  1.16 us
    ppermute x1, starting transfers between devices, shards(): moving = lax.ppermute(moving, 'ch', ring)  0.74 us
    convert_element_type x1, other arithmetic, shards(): return total.astype(BF16)  0.68 us
    ppermute x1, starting transfers between devices, shards(): two = lax.ppermute(own, ('seq', 'ch'), [(b, a) for a, b in ways])  0.49 us
  transfers between devices with their start and end apart: 3, of which 1 were waited for; matrix products, arithmetic and copies ran while one was open for 0% of the time, Pallas kernels for 24%

profile of v3, /device:TPU:0, one launch (start us, length us, event | category | flops | bytes accessed | tf_op | source)
XLA Modules:
  0.0 21.8 jit_solution(1723752041268270487)
XLA Ops:
  0.0 0.5 %collective-permute-start.1 = (s32[1,256]{1,0:T(1,128)}, s32[1,256]{1,0:T(1,128)S(1)}, u32[]{:S(2)}, u32[]{:S(2)}) collective-permute-start(s32[1,256]{1,0:T(1,128)} %bitcast.1), channel_id=1, source_target_pairs={{3,0},{0,1},{1,2},{4,3},{7,4},{2,5},{5,6},{8,7},{11,8},{6,9},{9,10... | collective-permute-start | bytes 3080 | tf_op jit(solution)/shard_map/ppermute | solution.py:332
  0.5 1.9 %collective-permute-start = (s32[1,256]{1,0:T(1,128)}, s32[1,256]{1,0:T(1,128)S(1)}, u32[]{:S(2)}, u32[]{:S(2)}) collective-permute-start(s32[1,256]{1,0:T(1,128)} %bitcast.2), channel_id=1, source_target_pairs={{0,3},{1,0},{2,1},{3,4},{4,7},{5,2},{6,5},{7,8},{8,11},{9,6},{10,9... | collective-permute-start | bytes 3080 | tf_op jit(solution)/shard_map/ppermute | solution.py:331
  2.4 5.3 %prepare.1 = (s32[1,256]{1,0:T(1,128)S(1)}, bf16[3,64,2048]{2,1,0:T(8,128)(2,1)S(1)}, bf16[18432,256]{1,0:T(8,128)(2,1)S(1)}, f32[24,2048]{1,0:T(8,128)S(1)}) custom-call(s32[1,256]{1,0:T(1,128)} %bitcast.3, bf16[3,4,2048]{2,1,0:T(4,128)(2,1)} %nuc_hbm.1, f32[3,7,2048]{2,1,0:T(8,128)} %sf_hbm.1, f32[128,128]{1,0:T(8,128)} %mr_hbm.1), custom_call_target="tpu_custom_call" | custom-call | flops 100000000 | bytes 10000000 | tf_op jit(solution)/shard_map/prepare/pallas_call | solution.py:307
  7.7 0.0 collective-permute-done.1.two_ref
  7.7 0.0 collective-permute-done.one_ref
  7.7 11.5 %annotate.1 = f32[256,256]{1,0:T(8,128)S(1)} custom-call(s32[1,256]{1,0:T(1,128)S(1)} %collective-permute-done.one_ref, s32[1,256]{1,0:T(1,128)S(1)} %get-tuple-element.9.own_ref, s32[1,256]{1,0:T(1,128)S(1)} %collective-permute-done.1.two_ref, bf16[3,64,2048]{2,1,0:T(8,128)(2,1)S(1)} %get-tuple-element.10.wn_ref, ...), custom_call_target="tpu_custom_call" | custom-call | flops 8000000000 | bytes 10000000 | tf_op jit(solution)/shard_map/annotate/pallas_call | solution.py:334
  19.2 0.7 %collective-permute-start.2 = (f32[256,256]{1,0:T(8,128)S(1)}, f32[256,256]{1,0:T(8,128)S(1)}, u32[]{:S(2)}, u32[]{:S(2)}) collective-permute-start(f32[256,256]{1,0:T(8,128)S(1)} %annotate.1), channel_id=1, source_target_pairs={{0,1},{1,0},{2,3},{3,2},{4,5},{5,4},{6,7},{7,6},{8,9},{9,8},{10,11... | collective-permute-start | bytes 786440 | tf_op jit(solution)/shard_map/ppermute | solution.py:358
  19.9 1.2 %collective-permute-done.2 = f32[256,256]{1,0:T(8,128)S(1)} collective-permute-done((f32[256,256]{1,0:T(8,128)S(1)}, f32[256,256]{1,0:T(8,128)S(1)}, u32[]{:S(2)}, u32[]{:S(2)}) %collective-permute-start.2) | collective-permute-done | bytes 262176 | tf_op jit(solution)/shard_map/ppermute | solution.py:358
  21.1 0.7 %add_convert_fusion = bf16[256,256]{1,0:T(8,128)(2,1)} fusion(f32[256,256]{1,0:T(8,128)S(1)} %annotate.1, f32[256,256]{1,0:T(8,128)S(1)} %collective-permute-done.2), kind=kLoop, calls=%fused_computation | loop fusion | flops 131072 | bytes 655360 | tf_op jit(solution)/shard_map/convert_element_type | solution.py:360
Async XLA Ops:
  0.0 7.7 %collective-permute-start.1 = (s32[1,256]{1,0:T(1,128)}, s32[1,256]{1,0:T(1,128)S(1)}, u32[]{:S(2)}, u32[]{:S(2)}) collective-permute-start(s32[1,256]{1,0:T(1,128)} %bitcast.1), channel_id=1, source_target_pairs={{3,0},{0,1},{1,2},{4,3},{7,4},{2,5},{5,6},{8,7},{11,8},{6,9},{9,10... | collective-permute-start | bytes 3080 | tf_op jit(solution)/shard_map/ppermute | solution.py:332
  0.5 7.2 %collective-permute-start = (s32[1,256]{1,0:T(1,128)}, s32[1,256]{1,0:T(1,128)S(1)}, u32[]{:S(2)}, u32[]{:S(2)}) collective-permute-start(s32[1,256]{1,0:T(1,128)} %bitcast.2), channel_id=1, source_target_pairs={{0,3},{1,0},{2,1},{3,4},{4,7},{5,2},{6,5},{7,8},{8,11},{9,6},{10,9... | collective-permute-start | bytes 3080 | tf_op jit(solution)/shard_map/ppermute | solution.py:331
  19.2 1.9 %collective-permute-start.2 = (f32[256,256]{1,0:T(8,128)S(1)}, f32[256,256]{1,0:T(8,128)S(1)}, u32[]{:S(2)}, u32[]{:S(2)}) collective-permute-start(f32[256,256]{1,0:T(8,128)S(1)} %annotate.1), channel_id=1, source_target_pairs={{0,1},{1,0},{2,3},{3,2},{4,5},{5,4},{6,7},{7,6},{8,9},{9,8},{10,11... | collective-permute-start | bytes 786440 | tf_op jit(solution)/shard_map/ppermute | solution.py:358

commit v4 on v3

--- a/solution.py
+++ b/solution.py
@@ -44,7 +44,7 @@
         self.window = 2 * taps
         self.offset = self.window - self.part - 2 * self.rim
         self.missing = taps - 1 - self.offset
-        self.mix_rows = up(self.part + 2 * self.rim, PACK)
+        self.mix_rows = up(self.part + 2 * self.rim, SUB)
         self.track_rows = (PARTS - 1) * self.part + self.mix_rows
         self.hot_rows = PACK + (PARTS - 1) * self.part + self.window
         self.lead = PACK + self.offset + self.rim + short_len - 1
@@ -81,28 +81,25 @@
     lax.fori_loop(0, nuc_ref.shape[2] // WIDE, step, 0)
 
 
-def build_mixers(plan, mr_ref, fr_ref, mixer_ref):
-    taps, rows = plan.taps, plan.mix_rows
-    total = iota((taps, taps), 0) + iota((taps, taps), 1)
-    turn = (total == plan.offset) | (total == plan.offset + taps)
+def build_turned(plan, mr_ref, fr_ref):
+    total = iota((plan.taps, plan.taps), 0) + iota((plan.taps, plan.taps), 1)
+    turn = (total == plan.offset) | (total == plan.offset + plan.taps)
     fr_ref[...] = dot(mr_ref[...].astype(BF16), ones_where(turn))
-    gap = iota((rows, taps), 0) - iota((rows, taps), 1)
-    near_mask = ones_where((gap <= plan.missing) & (gap >= -plan.offset))
-    far_mask = ones_where(gap > plan.missing)
-    filters = mr_ref.shape[0]
-
-    def step(b, carry):
-        block = fr_ref[pl.ds(pl.multiple_of(b * SUB, SUB), SUB), :]
-        for g in range(SUB):
-            wide = jnp.broadcast_to(block[g : g + 1], (taps, taps))
-            turned = pltpu.roll(wide, 0, 1, stride=1, stride_axis=0).astype(BF16)
-            turned = jnp.concatenate([turned, turned[: rows - taps]], axis=0)
-            at = pl.ds(pl.multiple_of((b * SUB + g) * rows, rows), rows)
-            mixer_ref[at, :taps] = turned * near_mask
-            mixer_ref[at, taps:] = turned * far_mask
-        return carry
-
-    lax.fori_loop(0, filters // SUB, step, 0)
+
+
+def build_masks(plan, mask_ref):
+    taps = plan.taps
+    gap = iota((plan.mix_rows, taps), 0) - iota((plan.mix_rows, taps), 1)
+    mask_ref[:, :taps] = ones_where((gap <= plan.missing) & (gap >= -plan.offset))
+    mask_ref[:, taps:] = ones_where(gap > plan.missing)
+
+
+def build_mixer(plan, taps_row, mask_ref):
+    taps = plan.taps
+    wide = jnp.broadcast_to(taps_row, (taps, taps))
+    turned = pltpu.roll(wide, 0, 1, stride=1, stride_axis=0).astype(BF16)
+    turned = jnp.concatenate([turned, turned[: plan.mix_rows - taps]], axis=0)
+    return turned * mask_ref[:, :taps], turned * mask_ref[:, taps:]
 
 
 def build_edges(plan, mr_ref, edge_ref):
@@ -126,15 +123,15 @@
 
 
 def prepare(
-    plan, own_hbm, nuc_hbm, sf_hbm, mr_hbm, own_ref, wn_ref, mixer_ref, edge_ref,
-    nuc_ref, sf_ref, mr_ref, fr_ref, sems,
+    plan, own_hbm, nuc_hbm, sf_hbm, mr_hbm, own_ref, wn_ref, fr_ref, edge_ref,
+    nuc_ref, sf_ref, mr_ref, sems,
 ):
     pairs = [(mr_hbm, mr_ref), (nuc_hbm, nuc_ref), (sf_hbm, sf_ref), (own_hbm, own_ref)]
     copies = [pltpu.make_async_copy(a, b, sems.at[i]) for i, (a, b) in enumerate(pairs)]
     for copy in copies:
         copy.start()
     copies[0].wait()
-    build_mixers(plan, mr_ref, fr_ref, mixer_ref)
+    build_turned(plan, mr_ref, fr_ref)
     build_edges(plan, mr_ref, edge_ref)
     for copy in copies[1:]:
         copy.wait()
@@ -190,17 +187,19 @@
 
 
 def kernel(
-    plan, count, one_ref, own_ref, two_ref, wn_ref, mixer_ref, edge_ref, hw_hbm, out_ref,
-    hw_ref, hot_ref, query_ref, data_now, edge_now, query_now, track_ref, score_ref, sem,
+    plan, count, one_ref, own_ref, two_ref, wn_ref, fr_ref, edge_ref, hw_hbm, out_ref,
+    hw_ref, hot_ref, query_ref, mask_ref, mixer_now, data_now, edge_now, query_now, track_ref, score_ref, sem,
 ):
     channels = wn_ref.shape[2]
     part, window, mix_rows = plan.part, plan.window, plan.mix_rows
-    group_width = channels * mix_rows // mixer_ref.shape[0]
+    group_width = channels // fr_ref.shape[0]
+    half_step = WIDE // group_width // 2
     tile_groups = HALF // group_width
     tile_rows = tile_groups * mix_rows
 
     fetch = pltpu.make_async_copy(hw_hbm, hw_ref, sem)
     fetch.start()
+    build_masks(plan, mask_ref)
     tok = coded_letters(plan, count, one_ref, own_ref, two_ref)
     build_onehot(plan, tok, hot_ref, query_ref)
 
@@ -210,9 +209,8 @@
 
     steps = channels // WIDE
 
-    def gate(v, s):
-        lanes = pl.ds(v * WIDE, WIDE)
-        slot = v % 2
+    def gate(v, slot, s):
+        lanes = pl.ds(pl.multiple_of(v * WIDE, WIDE), WIDE)
         hot = hot_ref[s]
         gated = dot(hot, wn_ref[1, :, lanes]) * dot(hot, wn_ref[2, :, lanes])
         query_now[slot, s] = dot(query_ref[s], wn_ref[0, :, lanes])
@@ -227,14 +225,22 @@
             data_now[slot, 2 * j, :, to] = jnp.where(low_half, a, b).astype(BF16)
             data_now[slot, 2 * j + 1, :, to] = jnp.where(low_half, b, a).astype(BF16)
 
-    def mix(v, j):
-        slot = v % 2
+    def arrange(v, slot, i):
+        first = pl.multiple_of((2 * v + i) * half_step, half_step)
+        block = fr_ref[pl.ds(first, half_step), :]
+        for g in range(half_step):
+            near, far = build_mixer(plan, block[g : g + 1], mask_ref)
+            at = (i * half_step + g) * mix_rows
+            mixer_now[slot, at : at + mix_rows, : plan.taps] = near
+            mixer_now[slot, at : at + mix_rows, plan.taps :] = far
+
+    def mix(v, slot, j):
         some = slice(j * LANES, (j + 1) * LANES)
-        to = pl.ds(v * WIDE + j * LANES, LANES)
+        to = pl.ds(pl.multiple_of(v * WIDE + j * LANES, LANES), LANES)
         mixed = []
         for h in range(2):
-            tile = v * (WIDE // HALF) + 2 * j + h
-            mixers = mixer_ref[pl.ds(tile * tile_rows, tile_rows), :]
+            at = (2 * j + h) * tile_rows
+            mixers = mixer_now[slot, at : at + tile_rows, :]
             data = data_now[slot, 2 * j + h]
             middle = tile_rows // 2
             pieces = jnp.concatenate([dot(mixers[:middle], data), dot(mixers[middle:], data)], axis=0)
@@ -257,12 +263,20 @@
                 track_ref[at : at + length, to] = (own * whole).astype(BF16)
 
     for s in range(STRANDS):
-        gate(0, s)
-    for v in range(steps):
-        for i in range(2):
-            if v + 1 < steps:
-                gate(v + 1, i)
-            mix(v, i)
+        gate(0, 0, s)
+        arrange(0, 0, s)
+
+    def pair(u, carry):
+        for slot in range(2):
+            v = 2 * u + slot
+            following = jnp.minimum(v + 1, steps - 1)
+            for i in range(2):
+                gate(following, 1 - slot, i)
+                arrange(following, 1 - slot, i)
+                mix(v, slot, i)
+        return carry
+
+    lax.fori_loop(0, steps // 2, pair, 0)
 
     fetch.wait()
     totals = [None, None]
@@ -304,12 +318,12 @@
     hbm = pl.BlockSpec(memory_space=pl.ANY)
 
     own = tokens.reshape(1, plan.rows)
-    own_here, weights, mixers, edges = pl.pallas_call(
+    own_here, weights, turned, edges = pl.pallas_call(
         functools.partial(prepare, plan),
         out_shape=(
             jax.ShapeDtypeStruct(own.shape, own.dtype),
             jax.ShapeDtypeStruct((3, plan.depth, channels), BF16),
-            jax.ShapeDtypeStruct((filters * plan.mix_rows, plan.window), BF16),
+            jax.ShapeDtypeStruct(mr_filter.shape, F32),
             jax.ShapeDtypeStruct((up(plan.missing, 1) * SUB, channels), F32),
         ),
         in_specs=[hbm] * 4,
@@ -317,7 +331,6 @@
         scratch_shapes=[
             pltpu.VMEM(nuc_table.shape, BF16),
             pltpu.VMEM(short_filter.shape, F32),
-            pltpu.VMEM(mr_filter.shape, F32),
             pltpu.VMEM(mr_filter.shape, F32),
             pltpu.SemaphoreType.DMA((4,)),
         ],
@@ -340,6 +353,8 @@
             pltpu.VMEM(head_weight.shape, BF16),
             pltpu.VMEM((STRANDS, plan.hot_rows, plan.depth), BF16),
             pltpu.VMEM((STRANDS, plan.track_rows, plan.depth), BF16),
+            pltpu.VMEM((plan.mix_rows, plan.window), BF16),
+            pltpu.VMEM((2, WIDE * filters // channels * plan.mix_rows, plan.window), BF16),
             pltpu.VMEM((2, WIDE // HALF, plan.window, WIDE), BF16),
             pltpu.VMEM((2, STRANDS, PARTS, SUB, WIDE), F32),
             pltpu.VMEM((2, STRANDS, plan.track_rows, WIDE), F32),
@@ -350,7 +365,7 @@
         compiler_params=pltpu.CompilerParams(vmem_limit_bytes=24 * MIB),
         cost_estimate=pl.CostEstimate(flops=8 * 10**9, bytes_accessed=10**7, transcendentals=0),
         name="annotate",
-    )(one, own_here, two, weights, mixers, edges, stay(head_weight))
+    )(one, own_here, two, weights, turned, edges, stay(head_weight))
 
     ring = [(i, (i + 1) % cores) for i in range(cores)]
     total, moving = partial, partial

time: 21.9 us -> 19.7 us (0.90)
  Pallas kernels: 16.8 us -> 13.7 us
  starting transfers between devices: 3.15 us -> 3.95 us
    pallas_call x1, Pallas kernels: 5.27 us -> 2.37 us  [shards(): pl.pallas_call(functools.partial(prepare, plan), out_shape=(jax.ShapeDtyp...]
    ppermute x1, starting transfers between devices: 0.74 us -> 1.54 us  [shards(): moving = lax.ppermute(moving, 'ch', ring)]
  transfers between devices with their start and end apart: 3 -> 3, of which waited for: 1 -> 1; matrix products, arithmetic and copies ran while one was open for 0% -> 0% of each run, Pallas kernels for 24% -> 12%
where the time goes in v4:
time: 19.7 us; the launch traced here: 19.6 us
  Pallas kernels  13.7 us (70%)
  starting transfers between devices  3.95 us (20%)
  waiting for transfers between devices  1.17 us (6%)
  other arithmetic  0.68 us (3%)
    pallas_call x1, Pallas kernels, shards(): pl.pallas_call(functools.partial(kernel, plan, count), out_shape=jax.Shap...  11.4 us
    pallas_call x1, Pallas kernels, shards(): pl.pallas_call(functools.partial(prepare, plan), out_shape=(jax.ShapeDtyp...  2.37 us
    ppermute x1, starting transfers between devices, shards(): one = lax.ppermute(own, ('seq', 'ch'), ways)  1.92 us
    ppermute x1, starting transfers between devices, shards(): moving = lax.ppermute(moving, 'ch', ring)  1.54 us
    ppermute x1, waiting for transfers between devices, shards(): moving = lax.ppermute(moving, 'ch', ring)  1.16 us
    convert_element_type x1, other arithmetic, shards(): return total.astype(BF16)  0.68 us
    ppermute x1, starting transfers between devices, shards(): two = lax.ppermute(own, ('seq', 'ch'), [(b, a) for a, b in ways])  0.49 us
  transfers between devices with their start and end apart: 3, of which 1 were waited for; matrix products, arithmetic and copies ran while one was open for 0% of the time, Pallas kernels for 12%

profile of v4, /device:TPU:0, one launch (start us, length us, event | category | flops | bytes accessed | tf_op | source)
XLA Modules:
  0.0 19.6 jit_solution(10673981236651345688)
XLA Ops:
  0.0 0.5 %collective-permute-start.1 = (s32[1,256]{1,0:T(1,128)}, s32[1,256]{1,0:T(1,128)S(1)}, u32[]{:S(2)}, u32[]{:S(2)}) collective-permute-start(s32[1,256]{1,0:T(1,128)} %bitcast.1), channel_id=1, source_target_pairs={{3,0},{0,1},{1,2},{4,3},{7,4},{2,5},{5,6},{8,7},{11,8},{6,9},{9,10... | collective-permute-start | bytes 3080 | tf_op jit(solution)/shard_map/ppermute | solution.py:345
  0.5 1.9 %collective-permute-start = (s32[1,256]{1,0:T(1,128)}, s32[1,256]{1,0:T(1,128)S(1)}, u32[]{:S(2)}, u32[]{:S(2)}) collective-permute-start(s32[1,256]{1,0:T(1,128)} %bitcast.2), channel_id=1, source_target_pairs={{0,3},{1,0},{2,1},{3,4},{4,7},{5,2},{6,5},{7,8},{8,11},{9,6},{10,9... | collective-permute-start | bytes 3080 | tf_op jit(solution)/shard_map/ppermute | solution.py:344
  2.4 2.4 %prepare.1 = (s32[1,256]{1,0:T(1,128)S(1)}, bf16[3,64,2048]{2,1,0:T(8,128)(2,1)S(1)}, f32[128,128]{1,0:T(8,128)S(1)}, f32[24,2048]{1,0:T(8,128)S(1)}) custom-call(s32[1,256]{1,0:T(1,128)} %bitcast.3, bf16[3,4,2048]{2,1,0:T(4,128)(2,1)} %nuc_hbm.1, f32[3,7,2048]{2,1,0:T(8,128)} %sf_hbm.1, f32[128,128]{1,0:T(8,128)} %mr_hbm.1), custom_call_target="tpu_custom_call" | custom-call | flops 100000000 | bytes 10000000 | tf_op jit(solution)/shard_map/prepare/pallas_call | solution.py:321
  4.8 0.0 collective-permute-done.1.two_ref
  4.8 0.0 collective-permute-done.one_ref
  4.8 11.4 %annotate.1 = f32[256,256]{1,0:T(8,128)S(1)} custom-call(s32[1,256]{1,0:T(1,128)S(1)} %collective-permute-done.one_ref, s32[1,256]{1,0:T(1,128)S(1)} %get-tuple-element.9.own_ref, s32[1,256]{1,0:T(1,128)S(1)} %collective-permute-done.1.two_ref, bf16[3,64,2048]{2,1,0:T(8,128)(2,1)S(1)} %get-tuple-element.10.wn_ref, f32[128,128]{1,0:T(8,128)S(1)} %get-tuple-element.11.fr_ref, ...), custom_call_target="tpu_custom_call" | custom-call | flops 8000000000 | bytes 10000000 | tf_op jit(solution)/shard_map/annotate/pallas_call | solution.py:347
  16.2 1.5 %collective-permute-start.2 = (f32[256,256]{1,0:T(8,128)S(1)}, f32[256,256]{1,0:T(8,128)S(1)}, u32[]{:S(2)}, u32[]{:S(2)}) collective-permute-start(f32[256,256]{1,0:T(8,128)S(1)} %annotate.1), channel_id=1, source_target_pairs={{0,1},{1,0},{2,3},{3,2},{4,5},{5,4},{6,7},{7,6},{8,9},{9,8},{10,11... | collective-permute-start | bytes 786440 | tf_op jit(solution)/shard_map/ppermute | solution.py:373
  17.7 1.2 %collective-permute-done.2 = f32[256,256]{1,0:T(8,128)S(1)} collective-permute-done((f32[256,256]{1,0:T(8,128)S(1)}, f32[256,256]{1,0:T(8,128)S(1)}, u32[]{:S(2)}, u32[]{:S(2)}) %collective-permute-start.2) | collective-permute-done | bytes 262176 | tf_op jit(solution)/shard_map/ppermute | solution.py:373
  18.9 0.7 %add_convert_fusion = bf16[256,256]{1,0:T(8,128)(2,1)} fusion(f32[256,256]{1,0:T(8,128)S(1)} %annotate.1, f32[256,256]{1,0:T(8,128)S(1)} %collective-permute-done.2), kind=kLoop, calls=%fused_computation | loop fusion | flops 131072 | bytes 655360 | tf_op jit(solution)/shard_map/convert_element_type | solution.py:375
Async XLA Ops:
  0.0 4.8 %collective-permute-start.1 = (s32[1,256]{1,0:T(1,128)}, s32[1,256]{1,0:T(1,128)S(1)}, u32[]{:S(2)}, u32[]{:S(2)}) collective-permute-start(s32[1,256]{1,0:T(1,128)} %bitcast.1), channel_id=1, source_target_pairs={{3,0},{0,1},{1,2},{4,3},{7,4},{2,5},{5,6},{8,7},{11,8},{6,9},{9,10... | collective-permute-start | bytes 3080 | tf_op jit(solution)/shard_map/ppermute | solution.py:345
  0.5 4.3 %collective-permute-start = (s32[1,256]{1,0:T(1,128)}, s32[1,256]{1,0:T(1,128)S(1)}, u32[]{:S(2)}, u32[]{:S(2)}) collective-permute-start(s32[1,256]{1,0:T(1,128)} %bitcast.2), channel_id=1, source_target_pairs={{0,3},{1,0},{2,1},{3,4},{4,7},{5,2},{6,5},{7,8},{8,11},{9,6},{10,9... | collective-permute-start | bytes 3080 | tf_op jit(solution)/shard_map/ppermute | solution.py:344
  16.2 2.7 %collective-permute-start.2 = (f32[256,256]{1,0:T(8,128)S(1)}, f32[256,256]{1,0:T(8,128)S(1)}, u32[]{:S(2)}, u32[]{:S(2)}) collective-permute-start(f32[256,256]{1,0:T(8,128)S(1)} %annotate.1), channel_id=1, source_target_pairs={{0,1},{1,0},{2,3},{3,2},{4,5},{5,4},{6,7},{7,6},{8,9},{9,8},{10,11... | collective-permute-start | bytes 786440 | tf_op jit(solution)/shard_map/ppermute | solution.py:373

commit v5 on v4

--- a/solution.py
+++ b/solution.py
@@ -90,16 +90,16 @@
 def build_masks(plan, mask_ref):
     taps = plan.taps
     gap = iota((plan.mix_rows, taps), 0) - iota((plan.mix_rows, taps), 1)
-    mask_ref[:, :taps] = ones_where((gap <= plan.missing) & (gap >= -plan.offset))
-    mask_ref[:, taps:] = ones_where(gap > plan.missing)
+    mask_ref[:, :taps] = ((gap <= plan.missing) & (gap >= -plan.offset)).astype(F32)
+    mask_ref[:, taps:] = (gap > plan.missing).astype(F32)
 
 
 def build_mixer(plan, taps_row, mask_ref):
     taps = plan.taps
     wide = jnp.broadcast_to(taps_row, (taps, taps))
-    turned = pltpu.roll(wide, 0, 1, stride=1, stride_axis=0).astype(BF16)
+    turned = pltpu.roll(wide, 0, 1, stride=1, stride_axis=0)
     turned = jnp.concatenate([turned, turned[: plan.mix_rows - taps]], axis=0)
-    return turned * mask_ref[:, :taps], turned * mask_ref[:, taps:]
+    return (jnp.concatenate([turned, turned], axis=1) * mask_ref[...]).astype(BF16)
 
 
 def build_edges(plan, mr_ref, edge_ref):
@@ -229,10 +229,8 @@
         first = pl.multiple_of((2 * v + i) * half_step, half_step)
         block = fr_ref[pl.ds(first, half_step), :]
         for g in range(half_step):
-            near, far = build_mixer(plan, block[g : g + 1], mask_ref)
             at = (i * half_step + g) * mix_rows
-            mixer_now[slot, at : at + mix_rows, : plan.taps] = near
-            mixer_now[slot, at : at + mix_rows, plan.taps :] = far
+            mixer_now[slot, at : at + mix_rows, :] = build_mixer(plan, block[g : g + 1], mask_ref)
 
     def mix(v, slot, j):
         some = slice(j * LANES, (j + 1) * LANES)
@@ -353,7 +351,7 @@
             pltpu.VMEM(head_weight.shape, BF16),
             pltpu.VMEM((STRANDS, plan.hot_rows, plan.depth), BF16),
             pltpu.VMEM((STRANDS, plan.track_rows, plan.depth), BF16),
-            pltpu.VMEM((plan.mix_rows, plan.window), BF16),
+            pltpu.VMEM((plan.mix_rows, plan.window), F32),
             pltpu.VMEM((2, WIDE * filters // channels * plan.mix_rows, plan.window), BF16),
             pltpu.VMEM((2, WIDE // HALF, plan.window, WIDE), BF16),
             pltpu.VMEM((2, STRANDS, PARTS, SUB, WIDE), F32),

time: 19.7 us -> 18.7 us (0.949)
  Pallas kernels: 13.7 us -> 12.7 us
    pallas_call x1, Pallas kernels: 11.4 us -> 10.4 us  [shards(): pl.pallas_call(functools.partial(kernel, plan, count), out_shape=jax.Shap...]
  transfers between devices with their start and end apart: 3 -> 3, of which waited for: 1 -> 1; matrix products, arithmetic and copies ran while one was open for 0% -> 0% of each run, Pallas kernels for 12% -> 13%
where the time goes in v5:
time: 18.7 us; the launch traced here: 18.6 us
  Pallas kernels  12.7 us (68%)
  starting transfers between devices  3.96 us (21%)
  waiting for transfers between devices  1.17 us (6%)
  other arithmetic  0.68 us (4%)
    pallas_call x1, Pallas kernels, shards(): pl.pallas_call(functools.partial(kernel, plan, count), out_shape=jax.Shap...  10.4 us
    pallas_call x1, Pallas kernels, shards(): pl.pallas_call(functools.partial(prepare, plan), out_shape=(jax.ShapeDtyp...  2.37 us
    ppermute x1, starting transfers between devices, shards(): one = lax.ppermute(own, ('seq', 'ch'), ways)  1.92 us
    ppermute x1, starting transfers between devices, shards(): moving = lax.ppermute(moving, 'ch', ring)  1.55 us
    ppermute x1, waiting for transfers between devices, shards(): moving = lax.ppermute(moving, 'ch', ring)  1.16 us
    convert_element_type x1, other arithmetic, shards(): return total.astype(BF16)  0.68 us
    ppermute x1, starting transfers between devices, shards(): two = lax.ppermute(own, ('seq', 'ch'), [(b, a) for a, b in ways])  0.49 us
  transfers between devices with their start and end apart: 3, of which 1 were waited for; matrix products, arithmetic and copies ran while one was open for 0% of the time, Pallas kernels for 13%

profile of v5, /device:TPU:0, one launch (start us, length us, event | category | flops | bytes accessed | tf_op | source)
XLA Modules:
  0.0 18.6 jit_solution(4198828987139875192)
XLA Ops:
  0.0 0.5 %collective-permute-start.1 = (s32[1,256]{1,0:T(1,128)}, s32[1,256]{1,0:T(1,128)S(1)}, u32[]{:S(2)}, u32[]{:S(2)}) collective-permute-start(s32[1,256]{1,0:T(1,128)} %bitcast.1), channel_id=1, source_target_pairs={{3,0},{0,1},{1,2},{4,3},{7,4},{2,5},{5,6},{8,7},{11,8},{6,9},{9,10... | collective-permute-start | bytes 3080 | tf_op jit(solution)/shard_map/ppermute | solution.py:343
  0.5 1.9 %collective-permute-start = (s32[1,256]{1,0:T(1,128)}, s32[1,256]{1,0:T(1,128)S(1)}, u32[]{:S(2)}, u32[]{:S(2)}) collective-permute-start(s32[1,256]{1,0:T(1,128)} %bitcast.2), channel_id=1, source_target_pairs={{0,3},{1,0},{2,1},{3,4},{4,7},{5,2},{6,5},{7,8},{8,11},{9,6},{10,9... | collective-permute-start | bytes 3080 | tf_op jit(solution)/shard_map/ppermute | solution.py:342
  2.4 2.4 %prepare.1 = (s32[1,256]{1,0:T(1,128)S(1)}, bf16[3,64,2048]{2,1,0:T(8,128)(2,1)S(1)}, f32[128,128]{1,0:T(8,128)S(1)}, f32[24,2048]{1,0:T(8,128)S(1)}) custom-call(s32[1,256]{1,0:T(1,128)} %bitcast.3, bf16[3,4,2048]{2,1,0:T(4,128)(2,1)} %nuc_hbm.1, f32[3,7,2048]{2,1,0:T(8,128)} %sf_hbm.1, f32[128,128]{1,0:T(8,128)} %mr_hbm.1), custom_call_target="tpu_custom_call" | custom-call | flops 100000000 | bytes 10000000 | tf_op jit(solution)/shard_map/prepare/pallas_call | solution.py:319
  4.8 0.0 collective-permute-done.1.two_ref
  4.8 0.0 collective-permute-done.one_ref
  4.8 10.4 %annotate.1 = f32[256,256]{1,0:T(8,128)S(1)} custom-call(s32[1,256]{1,0:T(1,128)S(1)} %collective-permute-done.one_ref, s32[1,256]{1,0:T(1,128)S(1)} %get-tuple-element.9.own_ref, s32[1,256]{1,0:T(1,128)S(1)} %collective-permute-done.1.two_ref, bf16[3,64,2048]{2,1,0:T(8,128)(2,1)S(1)} %get-tuple-element.10.wn_ref, f32[128,128]{1,0:T(8,128)S(1)} %get-tuple-element.11.fr_ref, ...), custom_call_target="tpu_custom_call" | custom-call | flops 8000000000 | bytes 10000000 | tf_op jit(solution)/shard_map/annotate/pallas_call | solution.py:345
  15.2 1.6 %collective-permute-start.2 = (f32[256,256]{1,0:T(8,128)S(1)}, f32[256,256]{1,0:T(8,128)S(1)}, u32[]{:S(2)}, u32[]{:S(2)}) collective-permute-start(f32[256,256]{1,0:T(8,128)S(1)} %annotate.1), channel_id=1, source_target_pairs={{0,1},{1,0},{2,3},{3,2},{4,5},{5,4},{6,7},{7,6},{8,9},{9,8},{10,11... | collective-permute-start | bytes 786440 | tf_op jit(solution)/shard_map/ppermute | solution.py:371
  16.7 1.2 %collective-permute-done.2 = f32[256,256]{1,0:T(8,128)S(1)} collective-permute-done((f32[256,256]{1,0:T(8,128)S(1)}, f32[256,256]{1,0:T(8,128)S(1)}, u32[]{:S(2)}, u32[]{:S(2)}) %collective-permute-start.2) | collective-permute-done | bytes 262176 | tf_op jit(solution)/shard_map/ppermute | solution.py:371
  17.9 0.7 %add_convert_fusion = bf16[256,256]{1,0:T(8,128)(2,1)} fusion(f32[256,256]{1,0:T(8,128)S(1)} %annotate.1, f32[256,256]{1,0:T(8,128)S(1)} %collective-permute-done.2), kind=kLoop, calls=%fused_computation | loop fusion | flops 131072 | bytes 655360 | tf_op jit(solution)/shard_map/convert_element_type | solution.py:373
Async XLA Ops:
  0.0 4.8 %collective-permute-start.1 = (s32[1,256]{1,0:T(1,128)}, s32[1,256]{1,0:T(1,128)S(1)}, u32[]{:S(2)}, u32[]{:S(2)}) collective-permute-start(s32[1,256]{1,0:T(1,128)} %bitcast.1), channel_id=1, source_target_pairs={{3,0},{0,1},{1,2},{4,3},{7,4},{2,5},{5,6},{8,7},{11,8},{6,9},{9,10... | collective-permute-start | bytes 3080 | tf_op jit(solution)/shard_map/ppermute | solution.py:343
  0.5 4.3 %collective-permute-start = (s32[1,256]{1,0:T(1,128)}, s32[1,256]{1,0:T(1,128)S(1)}, u32[]{:S(2)}, u32[]{:S(2)}) collective-permute-start(s32[1,256]{1,0:T(1,128)} %bitcast.2), channel_id=1, source_target_pairs={{0,3},{1,0},{2,1},{3,4},{4,7},{5,2},{6,5},{7,8},{8,11},{9,6},{10,9... | collective-permute-start | bytes 3080 | tf_op jit(solution)/shard_map/ppermute | solution.py:342
  15.2 2.7 %collective-permute-start.2 = (f32[256,256]{1,0:T(8,128)S(1)}, f32[256,256]{1,0:T(8,128)S(1)}, u32[]{:S(2)}, u32[]{:S(2)}) collective-permute-start(f32[256,256]{1,0:T(8,128)S(1)} %annotate.1), channel_id=1, source_target_pairs={{0,1},{1,0},{2,3},{3,2},{4,5},{5,4},{6,7},{7,6},{8,9},{9,8},{10,11... | collective-permute-start | bytes 786440 | tf_op jit(solution)/shard_map/ppermute | solution.py:371

commit v6 on v5

--- a/solution.py
+++ b/solution.py
@@ -264,17 +264,21 @@
         gate(0, 0, s)
         arrange(0, 0, s)
 
-    def pair(u, carry):
+    def both_slots(u, last):
         for slot in range(2):
             v = 2 * u + slot
-            following = jnp.minimum(v + 1, steps - 1)
             for i in range(2):
-                gate(following, 1 - slot, i)
-                arrange(following, 1 - slot, i)
+                if slot == 0 or not last:
+                    gate(v + 1, 1 - slot, i)
+                    arrange(v + 1, 1 - slot, i)
                 mix(v, slot, i)
+
+    def pair(u, carry):
+        both_slots(u, False)
         return carry
 
-    lax.fori_loop(0, steps // 2, pair, 0)
+    lax.fori_loop(0, steps // 2 - 1, pair, 0)
+    both_slots(steps // 2 - 1, True)
 
     fetch.wait()
     totals = [None, None]

time: 18.7 us -> 18.5 us (0.989)
  Pallas kernels: 12.7 us -> 12.5 us
    pallas_call x1, Pallas kernels: 10.4 us -> 10.1 us  [shards(): pl.pallas_call(functools.partial(kernel, plan, count), out_shape=jax.Shap...]
where the time goes in v6:
time: 18.5 us; the launch traced here: 18.3 us
  Pallas kernels  12.5 us (68%)
  starting transfers between devices  3.96 us (21%)
  waiting for transfers between devices  1.17 us (6%)
  other arithmetic  0.68 us (4%)
    pallas_call x1, Pallas kernels, shards(): pl.pallas_call(functools.partial(kernel, plan, count), out_shape=jax.Shap...  10.1 us
    pallas_call x1, Pallas kernels, shards(): pl.pallas_call(functools.partial(prepare, plan), out_shape=(jax.ShapeDtyp...  2.37 us
    ppermute x1, starting transfers between devices, shards(): one = lax.ppermute(own, ('seq', 'ch'), ways)  1.92 us
    ppermute x1, starting transfers between devices, shards(): moving = lax.ppermute(moving, 'ch', ring)  1.55 us
    ppermute x1, waiting for transfers between devices, shards(): moving = lax.ppermute(moving, 'ch', ring)  1.16 us
    convert_element_type x1, other arithmetic, shards(): return total.astype(BF16)  0.68 us
    ppermute x1, starting transfers between devices, shards(): two = lax.ppermute(own, ('seq', 'ch'), [(b, a) for a, b in ways])  0.49 us
  transfers between devices with their start and end apart: 3, of which 1 were waited for; matrix products, arithmetic and copies ran while one was open for 0% of the time, Pallas kernels for 13%

profile of v6, /device:TPU:0, one launch (start us, length us, event | category | flops | bytes accessed | tf_op | source)
XLA Modules:
  0.0 18.3 jit_solution(12379115749049399374)
XLA Ops:
  0.0 0.5 %collective-permute-start.1 = (s32[1,256]{1,0:T(1,128)}, s32[1,256]{1,0:T(1,128)S(1)}, u32[]{:S(2)}, u32[]{:S(2)}) collective-permute-start(s32[1,256]{1,0:T(1,128)} %bitcast.1), channel_id=1, source_target_pairs={{3,0},{0,1},{1,2},{4,3},{7,4},{2,5},{5,6},{8,7},{11,8},{6,9},{9,10... | collective-permute-start | bytes 3080 | tf_op jit(solution)/shard_map/ppermute | solution.py:347
  0.5 1.9 %collective-permute-start = (s32[1,256]{1,0:T(1,128)}, s32[1,256]{1,0:T(1,128)S(1)}, u32[]{:S(2)}, u32[]{:S(2)}) collective-permute-start(s32[1,256]{1,0:T(1,128)} %bitcast.2), channel_id=1, source_target_pairs={{0,3},{1,0},{2,1},{3,4},{4,7},{5,2},{6,5},{7,8},{8,11},{9,6},{10,9... | collective-permute-start | bytes 3080 | tf_op jit(solution)/shard_map/ppermute | solution.py:346
  2.4 2.4 %prepare.1 = (s32[1,256]{1,0:T(1,128)S(1)}, bf16[3,64,2048]{2,1,0:T(8,128)(2,1)S(1)}, f32[128,128]{1,0:T(8,128)S(1)}, f32[24,2048]{1,0:T(8,128)S(1)}) custom-call(s32[1,256]{1,0:T(1,128)} %bitcast.3, bf16[3,4,2048]{2,1,0:T(4,128)(2,1)} %nuc_hbm.1, f32[3,7,2048]{2,1,0:T(8,128)} %sf_hbm.1, f32[128,128]{1,0:T(8,128)} %mr_hbm.1), custom_call_target="tpu_custom_call" | custom-call | flops 100000000 | bytes 10000000 | tf_op jit(solution)/shard_map/prepare/pallas_call | solution.py:323
  4.8 0.0 collective-permute-done.1.two_ref
  4.8 0.0 collective-permute-done.one_ref
  4.8 10.1 %annotate.1 = f32[256,256]{1,0:T(8,128)S(1)} custom-call(s32[1,256]{1,0:T(1,128)S(1)} %collective-permute-done.one_ref, s32[1,256]{1,0:T(1,128)S(1)} %get-tuple-element.9.own_ref, s32[1,256]{1,0:T(1,128)S(1)} %collective-permute-done.1.two_ref, bf16[3,64,2048]{2,1,0:T(8,128)(2,1)S(1)} %get-tuple-element.10.wn_ref, f32[128,128]{1,0:T(8,128)S(1)} %get-tuple-element.11.fr_ref, ...), custom_call_target="tpu_custom_call" | custom-call | flops 8000000000 | bytes 10000000 | tf_op jit(solution)/shard_map/annotate/pallas_call | solution.py:349
  14.9 1.6 %collective-permute-start.2 = (f32[256,256]{1,0:T(8,128)S(1)}, f32[256,256]{1,0:T(8,128)S(1)}, u32[]{:S(2)}, u32[]{:S(2)}) collective-permute-start(f32[256,256]{1,0:T(8,128)S(1)} %annotate.1), channel_id=1, source_target_pairs={{0,1},{1,0},{2,3},{3,2},{4,5},{5,4},{6,7},{7,6},{8,9},{9,8},{10,11... | collective-permute-start | bytes 786440 | tf_op jit(solution)/shard_map/ppermute | solution.py:375
  16.5 1.2 %collective-permute-done.2 = f32[256,256]{1,0:T(8,128)S(1)} collective-permute-done((f32[256,256]{1,0:T(8,128)S(1)}, f32[256,256]{1,0:T(8,128)S(1)}, u32[]{:S(2)}, u32[]{:S(2)}) %collective-permute-start.2) | collective-permute-done | bytes 262176 | tf_op jit(solution)/shard_map/ppermute | solution.py:375
  17.7 0.7 %add_convert_fusion = bf16[256,256]{1,0:T(8,128)(2,1)} fusion(f32[256,256]{1,0:T(8,128)S(1)} %annotate.1, f32[256,256]{1,0:T(8,128)S(1)} %collective-permute-done.2), kind=kLoop, calls=%fused_computation | loop fusion | flops 131072 | bytes 655360 | tf_op jit(solution)/shard_map/convert_element_type | solution.py:377
Async XLA Ops:
  0.0 4.8 %collective-permute-start.1 = (s32[1,256]{1,0:T(1,128)}, s32[1,256]{1,0:T(1,128)S(1)}, u32[]{:S(2)}, u32[]{:S(2)}) collective-permute-start(s32[1,256]{1,0:T(1,128)} %bitcast.1), channel_id=1, source_target_pairs={{3,0},{0,1},{1,2},{4,3},{7,4},{2,5},{5,6},{8,7},{11,8},{6,9},{9,10... | collective-permute-start | bytes 3080 | tf_op jit(solution)/shard_map/ppermute | solution.py:347
  0.5 4.3 %collective-permute-start = (s32[1,256]{1,0:T(1,128)}, s32[1,256]{1,0:T(1,128)S(1)}, u32[]{:S(2)}, u32[]{:S(2)}) collective-permute-start(s32[1,256]{1,0:T(1,128)} %bitcast.2), channel_id=1, source_target_pairs={{0,3},{1,0},{2,1},{3,4},{4,7},{5,2},{6,5},{7,8},{8,11},{9,6},{10,9... | collective-permute-start | bytes 3080 | tf_op jit(solution)/shard_map/ppermute | solution.py:346
  14.9 2.7 %collective-permute-start.2 = (f32[256,256]{1,0:T(8,128)S(1)}, f32[256,256]{1,0:T(8,128)S(1)}, u32[]{:S(2)}, u32[]{:S(2)}) collective-permute-start(f32[256,256]{1,0:T(8,128)S(1)} %annotate.1), channel_id=1, source_target_pairs={{0,1},{1,0},{2,3},{3,2},{4,5},{5,4},{6,7},{7,6},{8,9},{9,8},{10,11... | collective-permute-start | bytes 786440 | tf_op jit(solution)/shard_map/ppermute | solution.py:375

commit v7 on v6

--- a/solution.py
+++ b/solution.py
@@ -99,7 +99,8 @@
     wide = jnp.broadcast_to(taps_row, (taps, taps))
     turned = pltpu.roll(wide, 0, 1, stride=1, stride_axis=0)
     turned = jnp.concatenate([turned, turned[: plan.mix_rows - taps]], axis=0)
-    return (jnp.concatenate([turned, turned], axis=1) * mask_ref[...]).astype(BF16)
+    near, far = turned * mask_ref[:, :taps], turned * mask_ref[:, taps:]
+    return jnp.concatenate([near, far], axis=1).astype(BF16)
 
 
 def build_edges(plan, mr_ref, edge_ref):
@@ -267,11 +268,15 @@
     def both_slots(u, last):
         for slot in range(2):
             v = 2 * u + slot
-            for i in range(2):
-                if slot == 0 or not last:
-                    gate(v + 1, 1 - slot, i)
-                    arrange(v + 1, 1 - slot, i)
-                mix(v, slot, i)
+            more = slot == 0 or not last
+            if more:
+                gate(v + 1, 1 - slot, 0)
+                arrange(v + 1, 1 - slot, 0)
+                gate(v + 1, 1 - slot, 1)
+            mix(v, slot, 0)
+            if more:
+                arrange(v + 1, 1 - slot, 1)
+            mix(v, slot, 1)
 
     def pair(u, carry):
         both_slots(u, False)

time: 18.5 us -> 18.2 us (0.984)
  Pallas kernels: 12.5 us -> 12.2 us
    pallas_call x1, Pallas kernels: 10.1 us -> 9.86 us  [shards(): pl.pallas_call(functools.partial(kernel, plan, count), out_shape=jax.Shap...]
where the time goes in v7:
time: 18.2 us; the launch traced here: 18.1 us
  Pallas kernels  12.2 us (67%)
  starting transfers between devices  3.96 us (22%)
  waiting for transfers between devices  1.17 us (6%)
  other arithmetic  0.68 us (4%)
    pallas_call x1, Pallas kernels, shards(): pl.pallas_call(functools.partial(kernel, plan, count), out_shape=jax.Shap...  9.86 us
    pallas_call x1, Pallas kernels, shards(): pl.pallas_call(functools.partial(prepare, plan), out_shape=(jax.ShapeDtyp...  2.37 us
    ppermute x1, starting transfers between devices, shards(): one = lax.ppermute(own, ('seq', 'ch'), ways)  1.92 us
    ppermute x1, starting transfers between devices, shards(): moving = lax.ppermute(moving, 'ch', ring)  1.55 us
    ppermute x1, waiting for transfers between devices, shards(): moving = lax.ppermute(moving, 'ch', ring)  1.16 us
    convert_element_type x1, other arithmetic, shards(): return total.astype(BF16)  0.68 us
    ppermute x1, starting transfers between devices, shards(): two = lax.ppermute(own, ('seq', 'ch'), [(b, a) for a, b in ways])  0.49 us
  transfers between devices with their start and end apart: 3, of which 1 were waited for; matrix products, arithmetic and copies ran while one was open for 0% of the time, Pallas kernels for 13%

profile of v7, /device:TPU:0, one launch (start us, length us, event | category | flops | bytes accessed | tf_op | source)
XLA Modules:
  0.0 18.1 jit_solution(11663784418857447618)
XLA Ops:
  0.0 0.5 %collective-permute-start.1 = (s32[1,256]{1,0:T(1,128)}, s32[1,256]{1,0:T(1,128)S(1)}, u32[]{:S(2)}, u32[]{:S(2)}) collective-permute-start(s32[1,256]{1,0:T(1,128)} %bitcast.1), channel_id=1, source_target_pairs={{3,0},{0,1},{1,2},{4,3},{7,4},{2,5},{5,6},{8,7},{11,8},{6,9},{9,10... | collective-permute-start | bytes 3080 | tf_op jit(solution)/shard_map/ppermute | solution.py:352
  0.5 1.9 %collective-permute-start = (s32[1,256]{1,0:T(1,128)}, s32[1,256]{1,0:T(1,128)S(1)}, u32[]{:S(2)}, u32[]{:S(2)}) collective-permute-start(s32[1,256]{1,0:T(1,128)} %bitcast.2), channel_id=1, source_target_pairs={{0,3},{1,0},{2,1},{3,4},{4,7},{5,2},{6,5},{7,8},{8,11},{9,6},{10,9... | collective-permute-start | bytes 3080 | tf_op jit(solution)/shard_map/ppermute | solution.py:351
  2.4 2.4 %prepare.1 = (s32[1,256]{1,0:T(1,128)S(1)}, bf16[3,64,2048]{2,1,0:T(8,128)(2,1)S(1)}, f32[128,128]{1,0:T(8,128)S(1)}, f32[24,2048]{1,0:T(8,128)S(1)}) custom-call(s32[1,256]{1,0:T(1,128)} %bitcast.3, bf16[3,4,2048]{2,1,0:T(4,128)(2,1)} %nuc_hbm.1, f32[3,7,2048]{2,1,0:T(8,128)} %sf_hbm.1, f32[128,128]{1,0:T(8,128)} %mr_hbm.1), custom_call_target="tpu_custom_call" | custom-call | flops 100000000 | bytes 10000000 | tf_op jit(solution)/shard_map/prepare/pallas_call | solution.py:328
  4.8 0.0 collective-permute-done.1.two_ref
  4.8 0.0 collective-permute-done.one_ref
  4.8 9.9 %annotate.1 = f32[256,256]{1,0:T(8,128)S(1)} custom-call(s32[1,256]{1,0:T(1,128)S(1)} %collective-permute-done.one_ref, s32[1,256]{1,0:T(1,128)S(1)} %get-tuple-element.9.own_ref, s32[1,256]{1,0:T(1,128)S(1)} %collective-permute-done.1.two_ref, bf16[3,64,2048]{2,1,0:T(8,128)(2,1)S(1)} %get-tuple-element.10.wn_ref, f32[128,128]{1,0:T(8,128)S(1)} %get-tuple-element.11.fr_ref, ...), custom_call_target="tpu_custom_call" | custom-call | flops 8000000000 | bytes 10000000 | tf_op jit(solution)/shard_map/annotate/pallas_call | solution.py:354
  14.7 1.6 %collective-permute-start.2 = (f32[256,256]{1,0:T(8,128)S(1)}, f32[256,256]{1,0:T(8,128)S(1)}, u32[]{:S(2)}, u32[]{:S(2)}) collective-permute-start(f32[256,256]{1,0:T(8,128)S(1)} %annotate.1), channel_id=1, source_target_pairs={{0,1},{1,0},{2,3},{3,2},{4,5},{5,4},{6,7},{7,6},{8,9},{9,8},{10,11... | collective-permute-start | bytes 786440 | tf_op jit(solution)/shard_map/ppermute | solution.py:380
  16.2 1.2 %collective-permute-done.2 = f32[256,256]{1,0:T(8,128)S(1)} collective-permute-done((f32[256,256]{1,0:T(8,128)S(1)}, f32[256,256]{1,0:T(8,128)S(1)}, u32[]{:S(2)}, u32[]{:S(2)}) %collective-permute-start.2) | collective-permute-done | bytes 262176 | tf_op jit(solution)/shard_map/ppermute | solution.py:380
  17.4 0.7 %add_convert_fusion = bf16[256,256]{1,0:T(8,128)(2,1)} fusion(f32[256,256]{1,0:T(8,128)S(1)} %annotate.1, f32[256,256]{1,0:T(8,128)S(1)} %collective-permute-done.2), kind=kLoop, calls=%fused_computation | loop fusion | flops 131072 | bytes 655360 | tf_op jit(solution)/shard_map/convert_element_type | solution.py:382
Async XLA Ops:
  0.0 4.8 %collective-permute-start.1 = (s32[1,256]{1,0:T(1,128)}, s32[1,256]{1,0:T(1,128)S(1)}, u32[]{:S(2)}, u32[]{:S(2)}) collective-permute-start(s32[1,256]{1,0:T(1,128)} %bitcast.1), channel_id=1, source_target_pairs={{3,0},{0,1},{1,2},{4,3},{7,4},{2,5},{5,6},{8,7},{11,8},{6,9},{9,10... | collective-permute-start | bytes 3080 | tf_op jit(solution)/shard_map/ppermute | solution.py:352
  0.5 4.3 %collective-permute-start = (s32[1,256]{1,0:T(1,128)}, s32[1,256]{1,0:T(1,128)S(1)}, u32[]{:S(2)}, u32[]{:S(2)}) collective-permute-start(s32[1,256]{1,0:T(1,128)} %bitcast.2), channel_id=1, source_target_pairs={{0,3},{1,0},{2,1},{3,4},{4,7},{5,2},{6,5},{7,8},{8,11},{9,6},{10,9... | collective-permute-start | bytes 3080 | tf_op jit(solution)/shard_map/ppermute | solution.py:351
  14.7 2.7 %collective-permute-start.2 = (f32[256,256]{1,0:T(8,128)S(1)}, f32[256,256]{1,0:T(8,128)S(1)}, u32[]{:S(2)}, u32[]{:S(2)}) collective-permute-start(f32[256,256]{1,0:T(8,128)S(1)} %annotate.1), channel_id=1, source_target_pairs={{0,1},{1,0},{2,3},{3,2},{4,5},{5,4},{6,7},{7,6},{8,9},{9,8},{10,11... | collective-permute-start | bytes 786440 | tf_op jit(solution)/shard_map/ppermute | solution.py:380

commit v8 on v7

--- a/solution.py
+++ b/solution.py
@@ -261,9 +261,10 @@
                 at = s * plan.track_rows + p * part
                 track_ref[at : at + length, to] = (own * whole).astype(BF16)
 
-    for s in range(STRANDS):
-        gate(0, 0, s)
-        arrange(0, 0, s)
+    arrange(0, 0, 0)
+    gate(0, 0, 0)
+    gate(0, 0, 1)
+    arrange(0, 0, 1)
 
     def both_slots(u, last):
         for slot in range(2):

time: 18.2 us -> 18.2 us (level)
  no operation moved by 1% of the time
where the time goes in v8:
time: 18.2 us; the launch traced here: 18 us
  Pallas kernels  12.2 us (67%)
  starting transfers between devices  3.96 us (22%)
  waiting for transfers between devices  1.17 us (6%)
  other arithmetic  0.68 us (4%)
    pallas_call x1, Pallas kernels, shards(): pl.pallas_call(functools.partial(kernel, plan, count), out_shape=jax.Shap...  9.84 us
    pallas_call x1, Pallas kernels, shards(): pl.pallas_call(functools.partial(prepare, plan), out_shape=(jax.ShapeDtyp...  2.37 us
    ppermute x1, starting transfers between devices, shards(): one = lax.ppermute(own, ('seq', 'ch'), ways)  1.92 us
    ppermute x1, starting transfers between devices, shards(): moving = lax.ppermute(moving, 'ch', ring)  1.55 us
    ppermute x1, waiting for transfers between devices, shards(): moving = lax.ppermute(moving, 'ch', ring)  1.16 us
    convert_element_type x1, other arithmetic, shards(): return total.astype(BF16)  0.68 us
    ppermute x1, starting transfers between devices, shards(): two = lax.ppermute(own, ('seq', 'ch'), [(b, a) for a, b in ways])  0.49 us
  transfers between devices with their start and end apart: 3, of which 1 were waited for; matrix products, arithmetic and copies ran while one was open for 0% of the time, Pallas kernels for 13%

profile of v8, /device:TPU:0, one launch (start us, length us, event | category | flops | bytes accessed | tf_op | source)
XLA Modules:
  0.0 18.0 jit_solution(17600536139168534982)
XLA Ops:
  0.0 0.5 %collective-permute-start.1 = (s32[1,256]{1,0:T(1,128)}, s32[1,256]{1,0:T(1,128)S(1)}, u32[]{:S(2)}, u32[]{:S(2)}) collective-permute-start(s32[1,256]{1,0:T(1,128)} %bitcast.1), channel_id=1, source_target_pairs={{3,0},{0,1},{1,2},{4,3},{7,4},{2,5},{5,6},{8,7},{11,8},{6,9},{9,10... | collective-permute-start | bytes 3080 | tf_op jit(solution)/shard_map/ppermute | solution.py:353
  0.5 1.9 %collective-permute-start = (s32[1,256]{1,0:T(1,128)}, s32[1,256]{1,0:T(1,128)S(1)}, u32[]{:S(2)}, u32[]{:S(2)}) collective-permute-start(s32[1,256]{1,0:T(1,128)} %bitcast.2), channel_id=1, source_target_pairs={{0,3},{1,0},{2,1},{3,4},{4,7},{5,2},{6,5},{7,8},{8,11},{9,6},{10,9... | collective-permute-start | bytes 3080 | tf_op jit(solution)/shard_map/ppermute | solution.py:352
  2.4 2.4 %prepare.1 = (s32[1,256]{1,0:T(1,128)S(1)}, bf16[3,64,2048]{2,1,0:T(8,128)(2,1)S(1)}, f32[128,128]{1,0:T(8,128)S(1)}, f32[24,2048]{1,0:T(8,128)S(1)}) custom-call(s32[1,256]{1,0:T(1,128)} %bitcast.3, bf16[3,4,2048]{2,1,0:T(4,128)(2,1)} %nuc_hbm.1, f32[3,7,2048]{2,1,0:T(8,128)} %sf_hbm.1, f32[128,128]{1,0:T(8,128)} %mr_hbm.1), custom_call_target="tpu_custom_call" | custom-call | flops 100000000 | bytes 10000000 | tf_op jit(solution)/shard_map/prepare/pallas_call | solution.py:329
  4.8 0.0 collective-permute-done.1.two_ref
  4.8 0.0 collective-permute-done.one_ref
  4.8 9.8 %annotate.1 = f32[256,256]{1,0:T(8,128)S(1)} custom-call(s32[1,256]{1,0:T(1,128)S(1)} %collective-permute-done.one_ref, s32[1,256]{1,0:T(1,128)S(1)} %get-tuple-element.9.own_ref, s32[1,256]{1,0:T(1,128)S(1)} %collective-permute-done.1.two_ref, bf16[3,64,2048]{2,1,0:T(8,128)(2,1)S(1)} %get-tuple-element.10.wn_ref, f32[128,128]{1,0:T(8,128)S(1)} %get-tuple-element.11.fr_ref, ...), custom_call_target="tpu_custom_call" | custom-call | flops 8000000000 | bytes 10000000 | tf_op jit(solution)/shard_map/annotate/pallas_call | solution.py:355
  14.7 1.6 %collective-permute-start.2 = (f32[256,256]{1,0:T(8,128)S(1)}, f32[256,256]{1,0:T(8,128)S(1)}, u32[]{:S(2)}, u32[]{:S(2)}) collective-permute-start(f32[256,256]{1,0:T(8,128)S(1)} %annotate.1), channel_id=1, source_target_pairs={{0,1},{1,0},{2,3},{3,2},{4,5},{5,4},{6,7},{7,6},{8,9},{9,8},{10,11... | collective-permute-start | bytes 786440 | tf_op jit(solution)/shard_map/ppermute | solution.py:381
  16.2 1.2 %collective-permute-done.2 = f32[256,256]{1,0:T(8,128)S(1)} collective-permute-done((f32[256,256]{1,0:T(8,128)S(1)}, f32[256,256]{1,0:T(8,128)S(1)}, u32[]{:S(2)}, u32[]{:S(2)}) %collective-permute-start.2) | collective-permute-done | bytes 262176 | tf_op jit(solution)/shard_map/ppermute | solution.py:381
  17.4 0.7 %add_convert_fusion = bf16[256,256]{1,0:T(8,128)(2,1)} fusion(f32[256,256]{1,0:T(8,128)S(1)} %annotate.1, f32[256,256]{1,0:T(8,128)S(1)} %collective-permute-done.2), kind=kLoop, calls=%fused_computation | loop fusion | flops 131072 | bytes 655360 | tf_op jit(solution)/shard_map/convert_element_type | solution.py:383
Async XLA Ops:
  0.0 4.8 %collective-permute-start.1 = (s32[1,256]{1,0:T(1,128)}, s32[1,256]{1,0:T(1,128)S(1)}, u32[]{:S(2)}, u32[]{:S(2)}) collective-permute-start(s32[1,256]{1,0:T(1,128)} %bitcast.1), channel_id=1, source_target_pairs={{3,0},{0,1},{1,2},{4,3},{7,4},{2,5},{5,6},{8,7},{11,8},{6,9},{9,10... | collective-permute-start | bytes 3080 | tf_op jit(solution)/shard_map/ppermute | solution.py:353
  0.5 4.3 %collective-permute-start = (s32[1,256]{1,0:T(1,128)}, s32[1,256]{1,0:T(1,128)S(1)}, u32[]{:S(2)}, u32[]{:S(2)}) collective-permute-start(s32[1,256]{1,0:T(1,128)} %bitcast.2), channel_id=1, source_target_pairs={{0,3},{1,0},{2,1},{3,4},{4,7},{5,2},{6,5},{7,8},{8,11},{9,6},{10,9... | collective-permute-start | bytes 3080 | tf_op jit(solution)/shard_map/ppermute | solution.py:352
  14.7 2.7 %collective-permute-start.2 = (f32[256,256]{1,0:T(8,128)S(1)}, f32[256,256]{1,0:T(8,128)S(1)}, u32[]{:S(2)}, u32[]{:S(2)}) collective-permute-start(f32[256,256]{1,0:T(8,128)S(1)} %annotate.1), channel_id=1, source_target_pairs={{0,1},{1,0},{2,3},{3,2},{4,5},{5,4},{6,7},{7,6},{8,9},{9,8},{10,11... | collective-permute-start | bytes 786440 | tf_op jit(solution)/shard_map/ppermute | solution.py:381
